TPU v7x, 32 devices: a whole 2x2x4 slice. The times are simulated.
32 devices in a mesh: user: 4 (over y, x), item: 8 (over z, core).
Axes of the slice: x: 2, y: 2, z: 4, core: 2. Of those that a mesh axis runs over, the one named last changes fastest.
Arguments:
- item_factors: bfloat16 [16384, 256], P('item'), may hold values from -0.125 to 0.125
- item_gram: float32 [256, 256], replicated, as said below
- tile_users: int32 [4, 8, 48], P('user', 'item'), may hold values from 0 to 3
- tile_items: int32 [4, 8, 48], P('user', 'item'), may hold values from 0 to 15, as said below
- tile_counts: int32 [4, 8], P('user', 'item'), may hold values from 12 to 48, as said below
- tile_values: bfloat16 [4, 8, 48, 128, 128], P('user', 'item'), may hold values from 0 to 8
Outputs:
- user_factors: float32 [2048, 256], P(('user', 'item'))
- item_rhs: float32 [8, 2048, 256], P('item', 'user')
Inputs may be any that keep to these rules, and one draw needn't show every extreme that they name: `item_gram`: symmetric positive definite. The pairs (tile_users, tile_items) of one device's slots are all different. `tile_counts`: some device uses all 48 slots in every draw.
All inputs are finite; a program needn't handle non-finite values.
Results may differ from a plain program's by a relative error of at most 0.0032.
Values may be sent and summed in bfloat16 or wider, within the bound.
A program may use at most 64 MiB of HBM per device.

v0:
```python
import functools

import jax
import jax.numpy as jnp
from jax import lax
from jax.experimental import pallas as pl
from jax.experimental.pallas import tpu as pltpu
from jax.sharding import PartitionSpec as P

USER_BLK = 4
ITERS = 3
CHUNK = 512
STREAMS = 2

epsilon = 1e-06
highest = lax.Precision.HIGHEST
MESH = pl.DeviceIdType.MESH
NT = (((1,), (1,)), ((), ()))


def confidence_of(w):
    w = w.astype(jnp.float32)
    return jnp.where(w > 0, 1.0 + w, 0.0).astype(jnp.bfloat16)


def kernel(
    nu, ni, scale,
    inv_ref, y_hbm, gram_hbm, tiles_hbm,
    sol_ref, item_ref,
    tiles, yv, gram, wide, wx, ct, xall, dirs, part, ra, sb, rb,
    d_state, r_state, x_state, n_state, i_state, sol_in,
    load_sem, w_send, w_recv, a_send, a_recv, b_send, b_recv,
    z_send, z_recv, f_send, f_recv, u_send, u_recv, s_send, s_recv, o_send, o_recv,
):
    slots, side, _ = tiles_hbm.shape
    items, rank = yv.shape
    group = wide.shape[0]
    rows = group // ni
    nz = ni // 2
    owners = nz // STREAMS
    low = (nz - owners) // 2
    stream_rows = group // STREAMS
    cols = items // nu
    blocks = items // side
    g, o = lax.axis_index("user"), lax.axis_index("item")
    z, c = lax.div(o, 2), lax.rem(o, 2)
    other = 1 - c
    sib = {"item": z * 2 + other}
    place = lax.rem(z - low + nz, owners)
    is_owner = (z >= low) & (z < low + owners)

    def znum(j):
        return lax.rem(z + (j + nz), nz)

    def unum(j):
        return lax.rem(g + (j + nu), nu)

    def zpeer(j):
        return {"item": znum(j) * 2 + c}

    def upeer(j):
        return {"user": unum(j)}

    def at_row(s, cc, q, base=0):
        return pl.ds(pl.multiple_of(base + ((s * 2 + cc) * owners + q) * rows, rows), rows)

    def half_rows(s, cc):
        size = owners * rows
        return pl.ds(pl.multiple_of((s * 2 + cc) * size, size), size)

    sent = []

    def rcopy(src, dst, ss, rs, dev):
        return pltpu.make_async_remote_copy(
            src_ref=src, dst_ref=dst, send_sem=ss, recv_sem=rs, device_id=dev, device_id_type=MESH
        )

    def send(*args):
        cp = rcopy(*args)
        cp.start()
        sent.append((None, cp))

    def send_if(cond, *args):
        cp = rcopy(*args)
        pl.when(cond)(cp.start)
        sent.append((cond, cp))

    def arrived(dst, ss, rs, dev):
        rcopy(dst, dst, ss, rs, dev).wait_recv()

    loads = [
        pltpu.make_async_copy(tiles_hbm, tiles.at[pl.ds(0, slots)], load_sem.at[0]),
        pltpu.make_async_copy(y_hbm, yv, load_sem.at[1]),
        pltpu.make_async_copy(gram_hbm, gram, load_sem.at[2]),
    ]
    for cp in loads:
        cp.start()

    barrier = pltpu.get_barrier_semaphore()
    pl.semaphore_signal(barrier, inc=1, device_id=sib, device_id_type=MESH)
    for j in range(1, nz):
        pl.semaphore_signal(barrier, inc=1, device_id=zpeer(j), device_id_type=MESH)
    for j in range(1, nu):
        pl.semaphore_signal(barrier, inc=1, device_id=upeer(j), device_id_type=MESH)

    tiles[slots] = jnp.zeros((side, side), jnp.bfloat16)
    loads[0].wait()
    for b in range(blocks):
        for q in range(owners):
            for s in range(STREAMS):
                for cc in range(2):
                    start = ((q * STREAMS + s) * 2 + cc) * rows
                    to = ((s * 2 + cc) * owners + q) * rows
                    u, off = start // side, start % side
                    wide[to : to + rows, b * side : (b + 1) * side] = tiles[
                        inv_ref[u * blocks + b], off : off + rows, :
                    ]
    for cp in loads[1:]:
        cp.wait()

    def wcol(gg):
        return pl.ds(pl.multiple_of(gg * cols, cols), cols)

    def turn(j):
        if j == 0:
            block = wide[:, wcol(g)]
        else:
            arrived(wx.at[j], w_send.at[j], w_recv.at[j], upeer(-j))
            block = wx[j]
        ct[j] = confidence_of(block).T

    turns = [[], [], [], []]
    for j in range(nu):
        turns[j * 4 // nu].append(j)

    def step_of(i):
        return pl.ds(pl.multiple_of(i * CHUNK, CHUNK), CHUNK)

    def stream_pass(k, s):
        here = slice(s * stream_rows, (s + 1) * stream_rows)

        def body(i, acc):
            at = step_of(i)
            yc = yv[at, :]
            if k == 0:
                weighted = confidence_of(wide[here, at])
            else:
                scores = lax.dot_general(dirs[k - 1, here], yc, NT, preferred_element_type=jnp.float32)
                weighted = (scores * wide[here, at].astype(jnp.float32)).astype(jnp.bfloat16)
            part[k, here] += jnp.dot(weighted, yc, preferred_element_type=jnp.float32)
            return acc

        part[k, here] = jnp.zeros((stream_rows, rank), jnp.float32)
        lax.fori_loop(0, items // CHUNK, body, 0, unroll=4)

    def reduce_start(k, s):
        arrived(ra.at[k, s], a_send.at[k, s], a_recv.at[k, s], sib)
        total = part[k, half_rows(s, c)] + ra[k, s]
        ra[k, s] = total
        sb[k, s] = total.astype(jnp.bfloat16)
        for q in range(owners):
            zo = q + low
            j = lax.rem(zo - z + nz, nz)
            piece = sb.at[k, s, pl.ds(q * rows, rows)]
            send_if(
                z != zo, piece, rb.at[k, s, j], b_send.at[k, s, q], b_recv.at[k, s, j], {"item": zo * 2 + c}
            )

    def reduce_end(k, s):
        own = ra[k, s, pl.ds(pl.multiple_of(place * rows, rows), rows)]
        for j in range(1, nz):
            arrived(rb.at[k, s, j], b_send.at[k, s, 0], b_recv.at[k, s, j], zpeer(-j))
            own = own + rb[k, s, j].astype(jnp.float32)
        return own

    def buffer(k):
        return (xall, g * group) if k == ITERS else (dirs.at[k], 0)

    def gather_start(k, s, value):
        buf, base = buffer(k)
        mine = at_row(s, c, place, base)
        buf[mine, :] = value.astype(jnp.bfloat16)

    def gather_send(k, s):
        buf, base = buffer(k)
        mine = at_row(s, c, place, base)
        for j in range(1, nz):
            send_if(
                is_owner, buf.at[mine], buf.at[mine], z_send.at[k, s, j], z_recv.at[k, s, place], zpeer(j)
            )

    def gather_pass(k, s):
        buf, base = buffer(k)
        for q in range(owners):
            zo = q + low
            piece = at_row(s, c, q, base)

            @pl.when(z != zo)
            def _():
                arrived(buf.at[piece], z_send.at[k, s, 0], z_recv.at[k, s, q], {"item": lax.rem(o + 2, ni)})

            if k == ITERS:
                for v in range(1, nu):
                    send(buf.at[piece], buf.at[piece], u_send.at[v, s, q], u_recv.at[v, s, q], upeer(v))
            send(buf.at[piece], buf.at[piece], f_send.at[k, s, q], f_recv.at[k, s, q], sib)

    def gather_end(k, s):
        buf, base = buffer(k)
        for q in range(owners):
            arrived(buf.at[at_row(s, other, q, base)], f_send.at[k, s, q], f_recv.at[k, s, q], sib)

    def turn_all(which):
        for j in turns[which]:
            turn(j)

    def update(k, s):
        total = reduce_end(k, s)
        if k == 0:
            r_state[s] = total
            d_state[s] = total
            x_state[s] = jnp.zeros_like(total)
            n_state[s] = jnp.sum(total * total, axis=1, keepdims=True)
            gather_start(k, s, total)
            return
        direction = d_state[s]
        image = i_state[s] + total
        norm = n_state[s]
        alpha = norm / (jnp.sum(direction * image, axis=1, keepdims=True) + epsilon)
        sol = x_state[s] + alpha * direction
        x_state[s] = sol
        if k == ITERS:
            gather_start(k, s, sol)
            return
        residual = r_state[s] - alpha * image
        r_state[s] = residual
        norm_next = jnp.sum(residual * residual, axis=1, keepdims=True)
        direction = residual + norm_next / (norm + epsilon) * direction
        d_state[s] = direction
        n_state[s] = norm_next
        gather_start(k, s, direction)

    def grams():
        for s in range(STREAMS):
            i_state[s] = jnp.dot(
                d_state[s], gram[...], precision=highest, preferred_element_type=jnp.float32
            )

    for k in range(ITERS + 1):
        for s in range(STREAMS):
            if k:
                gather_end(k - 1, s)
            stream_pass(k, s)
            if k == 0 and s == 0:
                pl.semaphore_wait(barrier, nz + nu - 1)
            send(part.at[k, half_rows(s, other)], ra.at[k, s], a_send.at[k, s], a_recv.at[k, s], sib)
        for s in range(STREAMS):
            reduce_start(k, s)
        if k == 0:
            for j in range(1, nu):
                send(wide.at[:, wcol(unum(j))], wx.at[j], w_send.at[j], w_recv.at[j], upeer(j))
        else:
            pl.when(is_owner)(grams)
        if k == 1:
            turn_all(0)
        elif k == 2:
            turn_all(1)
        elif k == ITERS:
            turn_all(2)
            turn_all(3)
        for s in range(STREAMS):
            pl.when(is_owner)(functools.partial(update, k, s))
            gather_send(k, s)
        for s in range(STREAMS):
            gather_pass(k, s)

    k = ITERS
    for q in range(owners):
        for s in range(STREAMS):
            target = q * STREAMS + s
            if target != q + low:
                send_if(
                    z == q + low, x_state.at[s], sol_in, o_send.at[s], o_recv, {"item": target * 2 + c}
                )

    def finish(v):
        src = unum(-v)
        for s in range(STREAMS):
            for q in range(owners):
                piece = xall.at[at_row(s, other, q, src * group)]
                if v:
                    arrived(piece, s_send.at[v, s, q], s_recv.at[v, s, q], sib)
                else:
                    arrived(piece, f_send.at[k, s, q], f_recv.at[k, s, q], sib)
        here = pl.ds(pl.multiple_of(src * group, group), group)
        return jnp.dot(ct[v], xall[here, :], preferred_element_type=jnp.float32)

    for v in range(1, nu):
        for s in range(STREAMS):
            for q in range(owners):
                piece = xall.at[at_row(s, c, q, unum(-v) * group)]
                arrived(piece, u_send.at[v, s, q], u_recv.at[v, s, q], upeer(-v))
                send(piece, piece, s_send.at[v, s, q], s_recv.at[v, s, q], sib)
        if v == 1:
            item_ref[...] = finish(0)
        else:
            item_ref[...] += finish(v - 1)

    for target in range(nz):
        owner = target // STREAMS + low

        @pl.when(z == target)
        def _():
            if owner == target:
                sol_ref[...] = x_state[target % STREAMS]
            else:
                arrived(sol_in, o_send.at[0], o_recv, {"item": owner * 2 + c})
                sol_ref[...] = sol_in[...]

    item_ref[...] = (item_ref[...] + finish(nu - 1)) * scale
    for cond, cp in sent:
        if cond is None:
            cp.wait_send()
        else:
            pl.when(cond)(cp.wait_send)


def place_outputs(sol_in, item_in, sol_out, item_out):
    sol_out[...] = sol_in[...]
    item_out[...] = item_in[...]


def make_local(nu, ni):
    def local(item_factors, item_gram, tile_users, tile_items, tile_counts, tile_values):
        items, rank = item_factors.shape
        slots, side = tile_values.shape[2], tile_values.shape[-1]
        blocks = items // side
        group = USER_BLK * side
        rows = group // ni
        nz = ni // 2
        owners = nz // STREAMS
        cols = items // nu
        at = jnp.arange(slots, dtype=jnp.int32)
        key = jnp.where(at < tile_counts[0, 0], tile_users[0, 0] * blocks + tile_items[0, 0], -1)
        match = key[None, :] == jnp.arange(USER_BLK * blocks, dtype=jnp.int32)[:, None]
        inv = slots - jnp.sum(jnp.where(match, slots - at[None, :], 0), axis=1)
        scale = float(nu * group) ** -0.5
        bf, f4 = jnp.bfloat16, jnp.float32
        dma = pltpu.SemaphoreType.DMA
        rounds = ITERS + 1
        anywhere = pl.BlockSpec(memory_space=pl.ANY)
        vmem = pl.BlockSpec(memory_space=pltpu.VMEM)
        sol, item = pl.pallas_call(
            functools.partial(kernel, nu, ni, scale),
            out_shape=(
                jax.ShapeDtypeStruct((rows, rank), f4),
                jax.ShapeDtypeStruct((cols, rank), f4),
            ),
            in_specs=[pl.BlockSpec(memory_space=pltpu.SMEM), anywhere, anywhere, anywhere],
            out_specs=(vmem, vmem),
            scratch_shapes=[
                pltpu.VMEM((slots + 1, side, side), bf),
                pltpu.VMEM((items, rank), bf),
                pltpu.VMEM((rank, rank), f4),
                pltpu.VMEM((group, items), bf),
                pltpu.VMEM((nu, group, cols), bf),
                pltpu.VMEM((nu, cols, group), bf),
                pltpu.VMEM((nu * group, rank), bf),
                pltpu.VMEM((ITERS, group, rank), bf),
                pltpu.VMEM((rounds, group, rank), f4),
                pltpu.VMEM((rounds, STREAMS, owners * rows, rank), f4),
                pltpu.VMEM((rounds, STREAMS, owners * rows, rank), bf),
                pltpu.VMEM((rounds, STREAMS, nz, rows, rank), bf),
                pltpu.VMEM((STREAMS, rows, rank), f4),
                pltpu.VMEM((STREAMS, rows, rank), f4),
                pltpu.VMEM((STREAMS, rows, rank), f4),
                pltpu.VMEM((STREAMS, rows, 1), f4),
                pltpu.VMEM((STREAMS, rows, rank), f4),
                pltpu.VMEM((rows, rank), f4),
                dma((3,)),
                dma((nu,)), dma((nu,)),
                dma((rounds, STREAMS)), dma((rounds, STREAMS)),
                dma((rounds, STREAMS, owners)), dma((rounds, STREAMS, nz)),
                dma((rounds, STREAMS, nz)), dma((rounds, STREAMS, owners)),
                dma((rounds, STREAMS, owners)), dma((rounds, STREAMS, owners)),
                dma((nu, STREAMS, owners)), dma((nu, STREAMS, owners)),
                dma((nu, STREAMS, owners)), dma((nu, STREAMS, owners)),
                dma((STREAMS,)), dma(()),
            ],
            compiler_params=pltpu.CompilerParams(collective_id=0, has_side_effects=True),
        )(inv, item_factors, item_gram, tile_values.reshape(slots, side, side))
        sol, item = pl.pallas_call(
            place_outputs,
            out_shape=(
                jax.ShapeDtypeStruct((rows, rank), f4),
                jax.ShapeDtypeStruct((cols, rank), f4),
            ),
            in_specs=[vmem, vmem],
            out_specs=(vmem, vmem),
        )(sol, item)
        return sol, item[None]

    return local


def solution(mesh):
    return jax.shard_map(
        make_local(mesh.shape["user"], mesh.shape["item"]),
        mesh=mesh,
        in_specs=(
            P("item", None),
            P(),
            P("user", "item", None),
            P("user", "item", None),
            P("user", "item"),
            P("user", "item", None, None, None),
        ),
        out_specs=(P(("user", "item"), None), P("item", "user", None)),
        check_vma=False,
    )
```

profile of v0, /device:TPU:0, one launch (start us, length us, event | category | flops | bytes accessed | tf_op | source)
XLA Modules:
  0.0 65.3 jit_solution(4137677747232133132)
XLA Ops:
  1.3 0.7 %compare_select_fusion = (s32[48]{0:T(128)S(1)}, s32[48]{0:T(128)S(1)}) fusion(s32[1,1,48]{2,1,0:T(1,128)} %param.9, s32[1,1,48]{2,1,0:T(1,128)} %param.8, s32[]{:T(128)} %bitcast.5), kind=kLoop, calls=%fused_computation.2 | loop fusion | flops 240 | bytes 772 | tf_op jit(solution)/shard_map/jit(_where)/select_n | solution.py:343
  2.0 0.1 select_reduce_fusion
  2.1 0.5 broadcast_subtract_fusion.inv_ref
  2.6 60.8 %shard_map.77 = (f32[64,256]{1,0:T(8,128)}, f32[512,256]{1,0:T(8,128)}) custom-call(s32[64]{0:T(128)} %broadcast_subtract_fusion.inv_ref, bf16[2048,256]{1,0:T(8,128)(2,1)} %y_hbm.1, f32[256,256]{1,0:T(8,128)} %gram_hbm.1, bf16[48,128,128]{2,1,0:T(8,128)(2,1)} %bitcast.6), custom_call_target="tpu_custom_call" | custom-call | tf_op jit(solution)/shard_map/pallas_call | solution.py:352
  63.4 1.9 %shard_map.78 = (f32[64,256]{1,0:T(8,128)}, f32[512,256]{1,0:T(8,128)}) custom-call(f32[64,256]{1,0:T(8,128)} %get-tuple-element.6.sol_in, f32[512,256]{1,0:T(8,128)} %get-tuple-element.7.item_in), custom_call_target="tpu_custom_call" | custom-call | tf_op jit(solution)/shard_map/pallas_call | solution.py:391
where the time goes:
time: 65.5 us; the launch traced here: 65.3 us
  Pallas kernels  62.7 us (96%)
  other arithmetic  1.29 us (2%)
  between operations  1.29 us (2%)
    pallas_call x1, Pallas kernels, local(): pl.pallas_call(functools.partial(kernel, nu, ni, scale), out_shape=(jax.S...  60.8 us
    pallas_call x1, Pallas kernels, local(): pl.pallas_call(place_outputs, out_shape=(jax.ShapeDtypeStruct((rows, rank...  1.91 us

commit v1 on v0

v1 whole, which is shorter than its diff:
```python
import functools

import jax
import jax.numpy as jnp
from jax import lax
from jax.experimental import pallas as pl
from jax.experimental.pallas import tpu as pltpu
from jax.sharding import PartitionSpec as P

USER_BLK = 4
ITERS = 3
CHUNK = 1024
LAST_CHUNK = 512
STREAMS = 2
LANES = 128

epsilon = 1e-06
highest = lax.Precision.HIGHEST
MESH = pl.DeviceIdType.MESH
NT = (((1,), (1,)), ((), ()))


def confidence_of(w):
    w = w.astype(jnp.float32)
    return jnp.where(w > 0, 1.0 + w, 0.0).astype(jnp.bfloat16)


def kernel(
    nu, ni, scale,
    inv_ref, y_hbm, gram_hbm, tiles_hbm,
    sol_ref, item_ref,
    tiles, yv, gram, wide, ws, wx, ct, xb, pa, ra, own, sb, rb,
    d_state, r_state, x_state, n_state, i_state, a_state, sol_in,
    scal, sums, coef, x2,
    load_sem, w_send, w_recv, a_send, a_recv, y_send, y_recv, b_send, b_recv,
    z_send, z_recv, f_send, f_recv, u_send, u_recv, s_send, s_recv, o_send, o_recv,
    c_send, c_recv, p_send, p_recv,
):
    slots, side, _ = tiles_hbm.shape
    items, rank = y_hbm.shape
    group = wide.shape[0]
    half = group // 2
    rows = group // ni
    nz = ni // 2
    owners = nz // STREAMS
    low = (nz - owners) // 2
    srows = owners * rows
    cols = items // nu
    blocks = items // side
    devices = nu * ni
    per = STREAMS * rows
    g, o = lax.axis_index("user"), lax.axis_index("item")
    z, c = lax.div(o, 2), lax.rem(o, 2)
    other = 1 - c
    me = g * ni + o
    sib = {"item": z * 2 + other}
    place = lax.rem(z - low + nz, owners)
    is_owner = (z >= low) & (z < low + owners)

    def unum(j):
        return lax.rem(g + (j + nu), nu)

    def zpeer(j):
        return {"item": lax.rem(z + (j + nz), nz) * 2 + c}

    def upeer(j):
        return {"user": unum(j)}

    def peer(i):
        return {"user": lax.rem(g + lax.div(i, ni), nu), "item": lax.rem(o + lax.rem(i, ni), ni)}

    def piece(s, q, hh=0):
        at = (hh * STREAMS + s) * srows
        if isinstance(q, int):
            return pl.ds(at + q * rows, rows)
        return pl.ds(pl.multiple_of(at + q * rows, rows), rows)

    sent = []

    def rcopy(src, dst, ss, rs, dev):
        return pltpu.make_async_remote_copy(
            src_ref=src, dst_ref=dst, send_sem=ss, recv_sem=rs, device_id=dev, device_id_type=MESH
        )

    def send(*args):
        cp = rcopy(*args)
        cp.start()
        sent.append((None, cp))

    def send_if(cond, *args):
        cp = rcopy(*args)
        pl.when(cond)(cp.start)
        sent.append((cond, cp))

    def arrived(dst, ss, rs, dev):
        rcopy(dst, dst, ss, rs, dev).wait_recv()

    loads = [
        pltpu.make_async_copy(tiles_hbm, tiles.at[pl.ds(0, slots)], load_sem.at[0]),
        pltpu.make_async_copy(y_hbm, yv.at[0], load_sem.at[1]),
        pltpu.make_async_copy(gram_hbm, gram, load_sem.at[2]),
    ]
    for cp in loads:
        cp.start()

    barrier = pltpu.get_barrier_semaphore()

    def greet(i, carry):
        pl.semaphore_signal(barrier, inc=1, device_id=peer(i), device_id_type=MESH)
        return carry

    lax.fori_loop(1, devices, greet, 0)

    tiles[slots] = jnp.zeros((side, side), jnp.bfloat16)
    loads[0].wait()
    for b in range(blocks):
        for q in range(owners):
            for s in range(STREAMS):
                start = (q * STREAMS + s) * 2 * rows
                u, off = start // side, start % side
                for hh in range(2):
                    to = ((hh * STREAMS + s) * owners + q) * rows
                    at = pl.ds(pl.multiple_of(off + (c if hh == 0 else other) * rows, rows), rows)
                    wide[to : to + rows, b * side : (b + 1) * side] = tiles[
                        slots - inv_ref[u * blocks + b], at, :
                    ]
    for cp in loads[1:]:
        cp.wait()

    def wcol(gg):
        return pl.ds(pl.multiple_of(gg * cols, cols), cols)

    def turn(j):
        if j == 0:
            block = wide[:, wcol(g)]
        else:
            arrived(wx.at[j], w_send.at[j], w_recv.at[j], upeer(-j))
            block = wx[j]
        ct[j] = confidence_of(block).T

    turns = [[], [], [], []]
    for j in range(nu):
        turns[j * 4 // nu].append(j)

    def turn_all(which):
        for j in turns[which]:
            turn(j)

    def rhs_pass(hh):
        here = slice(hh * half, (hh + 1) * half)
        acc = jnp.zeros((half, rank), jnp.float32)
        for i in range(items // CHUNK):
            at = slice(i * CHUNK, (i + 1) * CHUNK)
            acc = acc + jnp.dot(
                confidence_of(wide[here, at]), yv[0, at, :], preferred_element_type=jnp.float32
            )
        return acc

    def stream_pass(k, s):
        here = slice(s * srows, (s + 1) * srows)
        acc = jnp.zeros((srows, rank), jnp.float32)
        for side_of, w_ref in enumerate((wide, ws)):
            for i in range(items // CHUNK):
                at = slice(i * CHUNK, (i + 1) * CHUNK)
                yc = yv[side_of, at, :]
                scores = lax.dot_general(xb[k - 1, 0, here, :], yc, NT, preferred_element_type=jnp.float32)
                weighted = (scores * w_ref[here, at].astype(jnp.float32)).astype(jnp.bfloat16)
                acc = acc + jnp.dot(weighted, yc, preferred_element_type=jnp.float32)
        return acc

    def last_pass():
        acc = jnp.zeros((half, LANES), jnp.float32)
        for side_of, w_ref in enumerate((wide, ws)):
            for i in range(items // LAST_CHUNK):
                at = slice(i * LAST_CHUNK, (i + 1) * LAST_CHUNK)
                scores = lax.dot_general(
                    xb[ITERS - 1, 0, 0:half, :], yv[side_of, at, :], NT, preferred_element_type=jnp.float32
                )
                weighted = (scores * w_ref[0:half, at].astype(jnp.float32)).astype(jnp.bfloat16)
                prod = weighted.astype(jnp.float32) * scores
                for j in range(LAST_CHUNK // LANES):
                    acc = acc + prod[:, j * LANES : (j + 1) * LANES]
        for q in range(owners):
            mine = [acc[(s * owners + q) * rows : (s * owners + q + 1) * rows] for s in range(STREAMS)]
            sums[me, q : q + 1, 0:per] = jnp.sum(jnp.concatenate(mine, axis=0).T, axis=0, keepdims=True)

    def reduce_start(k, s, total):
        own[s] = total
        sb[k, s] = total.astype(jnp.bfloat16)
        for q in range(owners):
            zo = q + low
            j = lax.rem(zo - z + nz, nz)
            part = sb.at[k, s, pl.ds(q * rows, rows)]
            send_if(
                z != zo, part, rb.at[k, s, j], b_send.at[k, s, q], b_recv.at[k, s, j], {"item": zo * 2 + c}
            )

    def reduce_end(k, s):
        total = own[s, pl.ds(pl.multiple_of(place * rows, rows), rows), :]
        for j in range(1, nz):
            arrived(rb.at[k, s, j], b_send.at[k, s, 0], b_recv.at[k, s, j], zpeer(-j))
            total = total + rb[k, s, j].astype(jnp.float32)
        return total

    def gather_send(k, s):
        mine = xb.at[k, 0, piece(s, place)]
        for j in range(1, nz):
            send_if(is_owner, mine, mine, z_send.at[k, s, j], z_recv.at[k, s, place], zpeer(j))

    def gather_end(k, s, pass_on):
        for q in range(owners):
            zo = q + low
            got = xb.at[k, 0, piece(s, q)]

            @pl.when(z != zo)
            def _():
                arrived(got, z_send.at[k, s, 0], z_recv.at[k, s, q], {"item": lax.rem(o + 2, ni)})

            if pass_on:
                for v in range(1, nu):
                    send(got, xb.at[k, v, piece(s, q)], u_send.at[k, v, s, q], u_recv.at[k, v, s, q], upeer(v))
                send(got, xb.at[k, 0, piece(s, q, 1)], f_send.at[k, s, q], f_recv.at[k, s, q], sib)

    mine_all, theirs_all = pl.ds(0, half), pl.ds(half, half)

    def basis_send(k):
        mine = xb.at[k, 0, mine_all]
        for v in range(1, nu):
            send(mine, xb.at[k, v, mine_all], u_send.at[k, v, 0, 0], u_recv.at[k, v, 0, 0], upeer(v))
        send(mine, xb.at[k, 0, theirs_all], f_send.at[k, 0, 0], f_recv.at[k, 0, 0], sib)

    def basis_pass(k):
        for v in range(1, nu):
            got = xb.at[k, v, mine_all]
            arrived(got, u_send.at[k, v, 0, 0], u_recv.at[k, v, 0, 0], upeer(-v))
            send(got, xb.at[k, v, theirs_all], s_send.at[k, v, 0, 0], s_recv.at[k, v, 0, 0], sib)

    def basis_end(k):
        arrived(xb.at[k, 0, theirs_all], f_send.at[k, 0, 0], f_recv.at[k, 0, 0], sib)
        for v in range(1, nu):
            arrived(xb.at[k, v, theirs_all], s_send.at[k, v, 0, 0], s_recv.at[k, v, 0, 0], sib)

    def update(k, s):
        total = reduce_end(k, s)
        if k == 0:
            r_state[s] = total
            d_state[s] = total
            n_state[s] = jnp.sum(total * total, axis=1, keepdims=True)
            xb[k, 0, piece(s, place), :] = total.astype(jnp.bfloat16)
            return
        direction = d_state[s]
        image = i_state[s] + total
        norm = n_state[s]
        alpha = norm / (jnp.sum(direction * image, axis=1, keepdims=True) + epsilon)
        residual = r_state[s] - alpha * image
        norm_next = jnp.sum(residual * residual, axis=1, keepdims=True)
        direction_next = residual + norm_next / (norm + epsilon) * direction
        xb[k, 0, piece(s, place), :] = direction_next.astype(jnp.bfloat16)
        moved = alpha * direction
        x_state[s] = moved if k == 1 else x_state[s] + moved
        a_state[k - 1, s] = alpha
        r_state[s] = residual
        d_state[s] = direction_next
        n_state[s] = norm_next

    def grams():
        for s in range(STREAMS):
            i_state[s] = jnp.dot(
                d_state[s], gram[...], precision=highest, preferred_element_type=jnp.float32
            )

    def spread(src, ss, rs):
        def body(i, carry):
            rcopy(src, src, ss.at[i], rs, peer(i)).start()
            return carry

        lax.fori_loop(1, devices, body, 0)

    def spread_end(src, ss, rs):
        def body(i, carry):
            rcopy(src, src, ss.at[i], rs, peer(i)).wait_send()
            return carry

        lax.fori_loop(1, devices, body, 0)

    my_scal = scal.at[(g * owners + place) * 2 + c]

    def tell():
        grams()
        lane = lax.broadcasted_iota(jnp.int32, (rows, LANES), 1)
        parts = []
        for s in range(STREAMS):
            turned = jnp.sum(d_state[s] * i_state[s], axis=1, keepdims=True)
            at = jnp.where(lane == 2, n_state[s], turned)
            at = jnp.where(lane == 1, a_state[1, s], at)
            parts.append(jnp.where(lane == 0, a_state[0, s], at))
        my_scal[:, 0:per] = jnp.concatenate(parts, axis=0).T[0:8]
        spread(my_scal, c_send, c_recv)

    pa[...] = rhs_pass(1)
    pl.semaphore_wait(barrier, devices - 1)
    for s in range(STREAMS):
        here = pl.ds(s * srows, srows)
        send(pa.at[here], ra.at[here], a_send.at[s], a_recv.at[s], sib)
    first = rhs_pass(0)
    for s in range(STREAMS):
        own[s] = first[s * srows : (s + 1) * srows]
    send(yv.at[0], yv.at[1], y_send.at[0], y_recv.at[0], sib)
    send(wide.at[theirs_all], ws, y_send.at[1], y_recv.at[1], sib)
    for s in range(STREAMS):
        here = pl.ds(s * srows, srows)
        arrived(ra.at[here], a_send.at[s], a_recv.at[s], sib)
        reduce_start(0, s, own[s] + ra[here, :])
    for j in range(1, nu):
        send(wide.at[:, wcol(unum(j))], wx.at[j], w_send.at[j], w_recv.at[j], upeer(j))
    turn_all(0)
    for s in range(STREAMS):
        pl.when(is_owner)(functools.partial(update, 0, s))
        gather_send(0, s)
    arrived(yv.at[1], y_send.at[0], y_recv.at[0], sib)
    arrived(ws, y_send.at[1], y_recv.at[1], sib)

    for k in range(1, ITERS):
        for s in range(STREAMS):
            gather_end(k - 1, s, False)
            reduce_start(k, s, stream_pass(k, s))
        basis_send(k - 1)
        pl.when(is_owner)(grams)
        if k == 1:
            turn_all(1)
        if k == 2:
            basis_pass(0)
        for s in range(STREAMS):
            pl.when(is_owner)(functools.partial(update, k, s))
            gather_send(k, s)

    pl.when(is_owner)(tell)
    for q in range(owners):
        for s in range(STREAMS):
            target = q * STREAMS + s
            if target != q + low:
                send_if(
                    z == q + low, x_state.at[s], sol_in, o_send.at[s], o_recv, {"item": target * 2 + c}
                )
    k = ITERS - 1
    for s in range(STREAMS):
        gather_end(k, s, True)
    last_pass()
    spread(sums.at[me], p_send, p_recv)

    basis_pass(1)
    turn_all(2)
    turn_all(3)
    known = scal.shape[0]

    @pl.when(is_owner)
    def _():
        every = scal.at[pl.ds(0, known - 1)]
        arrived(every, c_send.at[0], c_recv, sib)

    @pl.when(jnp.logical_not(is_owner))
    def _():
        arrived(scal, c_send.at[0], c_recv, sib)

    def cell(v, hh, q):
        return (v * 2 + hh) * owners + q

    def cells():
        for v in range(nu):
            for hh in range(2):
                for q in range(owners):
                    yield v, hh, q, unum(-v), (c if hh == 0 else other)

    def block(v, hh, s, q):
        at = ((hh * STREAMS + s) * owners + q) * rows
        return slice(at, at + rows)

    for v, hh, q, gv, cc in cells():
        n = cell(v, hh, q)
        coef[0:4, n, :] = scal[(gv * owners + q) * 2 + cc][0:4]
    alpha1, alpha2 = coef[0].T, coef[1].T
    for j in range(2):
        basis_end(j)
    for v, hh, q, gv, cc in cells():
        n = cell(v, hh, q)
        for s in range(STREAMS):
            at = block(v, hh, s, q)
            r = slice(s * rows, (s + 1) * rows)
            x2[v, at, :] = alpha1[r, n : n + 1] * xb[0, v, at, :].astype(jnp.float32) + alpha2[
                r, n : n + 1
            ] * xb[1, v, at, :].astype(jnp.float32)

    for v in range(1, nu):
        for s in range(STREAMS):
            for q in range(owners):
                got = xb.at[k, v, piece(s, q)]
                arrived(got, u_send.at[k, v, s, q], u_recv.at[k, v, s, q], upeer(-v))
                send(got, xb.at[k, v, piece(s, q, 1)], s_send.at[k, v, s, q], s_recv.at[k, v, s, q], sib)

    arrived(sums.at[pl.ds(0, devices - 1)], p_send.at[0], p_recv, sib)
    for v, hh, q, gv, cc in cells():
        n = cell(v, hh, q)
        total = coef[3, n : n + 1, :]
        for zz in range(nz):
            total = total + sums[gv * ni + zz * 2 + cc, q : q + 1, :]
        coef[4, n : n + 1, :] = coef[2, n : n + 1, :] / (total + epsilon)
    alpha3 = coef[4].T

    for target in range(nz):
        owner = target // STREAMS + low
        s, q = target % STREAMS, target // STREAMS

        @pl.when(z == target)
        def _():
            if owner == target:
                before = x_state[s]
            else:
                arrived(sol_in, o_send.at[0], o_recv, {"item": owner * 2 + c})
                before = sol_in[...]
            n = cell(0, 0, q)
            sol_ref[...] = before + alpha3[s * rows : (s + 1) * rows, n : n + 1] * xb[
                k, 0, block(0, 0, s, q), :
            ].astype(jnp.float32)

    for v in range(nu):
        total = None
        for hh in range(2):
            parts = []
            for s in range(STREAMS):
                for q in range(owners):
                    if hh == 1:
                        got = xb.at[k, v, piece(s, q, 1)]
                        if v:
                            arrived(got, s_send.at[k, v, s, q], s_recv.at[k, v, s, q], sib)
                        else:
                            arrived(got, f_send.at[k, s, q], f_recv.at[k, s, q], sib)
                    n = cell(v, hh, q)
                    at = block(v, hh, s, q)
                    parts.append(
                        x2[v, at, :]
                        + alpha3[s * rows : (s + 1) * rows, n : n + 1] * xb[k, v, at, :].astype(jnp.float32)
                    )
            final = jnp.concatenate(parts, axis=0).astype(jnp.bfloat16)
            term = jnp.dot(
                ct[v, :, hh * half : (hh + 1) * half], final, preferred_element_type=jnp.float32
            )
            total = term if total is None else total + term
        if v == 0:
            item_ref[...] = total
        elif v < nu - 1:
            item_ref[...] += total
        else:
            item_ref[...] = (item_ref[...] + total) * scale

    for cond, cp in sent:
        if cond is None:
            cp.wait_send()
        else:
            pl.when(cond)(cp.wait_send)
    spread_end(sums.at[me], p_send, p_recv)
    pl.when(is_owner)(functools.partial(spread_end, my_scal, c_send, c_recv))


def place_outputs(sol_in, item_in, sol_out, item_out):
    sol_out[...] = sol_in[...]
    item_out[...] = item_in[...]


def make_local(nu, ni):
    def local(item_factors, item_gram, tile_users, tile_items, tile_counts, tile_values):
        items, rank = item_factors.shape
        slots, side = tile_values.shape[2], tile_values.shape[-1]
        blocks = items // side
        group = USER_BLK * side
        half = group // 2
        rows = group // ni
        nz = ni // 2
        owners = nz // STREAMS
        srows = owners * rows
        cols = items // nu
        at = jnp.arange(slots, dtype=jnp.int32)
        cell = jnp.arange(USER_BLK * blocks, dtype=jnp.int32)[:, None]
        match = (
            (tile_users[0] == cell // blocks) & (tile_items[0] == cell % blocks) & (at[None, :] < tile_counts[0, 0])
        )
        inv = jnp.sum(jnp.where(match, slots - at[None, :], 0), axis=1)
        scale = float(nu * group) ** -0.5
        bf, f4 = jnp.bfloat16, jnp.float32
        dma = pltpu.SemaphoreType.DMA
        vm = pltpu.VMEM
        cells = max(8, nu * 2 * owners)
        anywhere = pl.BlockSpec(memory_space=pl.ANY)
        vmem = pl.BlockSpec(memory_space=pltpu.VMEM)
        sol, item = pl.pallas_call(
            functools.partial(kernel, nu, ni, scale),
            out_shape=(
                jax.ShapeDtypeStruct((rows, rank), f4),
                jax.ShapeDtypeStruct((cols, rank), f4),
            ),
            in_specs=[pl.BlockSpec(memory_space=pltpu.SMEM), anywhere, anywhere, anywhere],
            out_specs=(vmem, vmem),
            scratch_shapes=[
                vm((slots + 1, side, side), bf),
                vm((2, items, rank), bf),
                vm((rank, rank), f4),
                vm((group, items), bf),
                vm((half, items), bf),
                vm((nu, group, cols), bf),
                vm((nu, cols, group), bf),
                vm((ITERS, nu, group, rank), bf),
                vm((half, rank), f4),
                vm((half, rank), f4),
                vm((STREAMS, srows, rank), f4),
                vm((ITERS, STREAMS, srows, rank), bf),
                vm((ITERS, STREAMS, nz, rows, rank), bf),
                vm((STREAMS, rows, rank), f4),
                vm((STREAMS, rows, rank), f4),
                vm((STREAMS, rows, rank), f4),
                vm((STREAMS, rows, 1), f4),
                vm((STREAMS, rows, rank), f4),
                vm((2, STREAMS, rows, 1), f4),
                vm((rows, rank), f4),
                vm((nu * owners * 2, 8, LANES), f4),
                vm((nu * ni, owners, LANES), f4),
                vm((5, cells, LANES), f4),
                vm((nu, group, rank), f4),
                dma((3,)),
                dma((nu,)), dma((nu,)),
                dma((STREAMS,)), dma((STREAMS,)),
                dma((2,)), dma((2,)),
                dma((ITERS, STREAMS, owners)), dma((ITERS, STREAMS, nz)),
                dma((ITERS, STREAMS, nz)), dma((ITERS, STREAMS, owners)),
                dma((ITERS, STREAMS, owners)), dma((ITERS, STREAMS, owners)),
                dma((ITERS, nu, STREAMS, owners)), dma((ITERS, nu, STREAMS, owners)),
                dma((ITERS, nu, STREAMS, owners)), dma((ITERS, nu, STREAMS, owners)),
                dma((STREAMS,)), dma(()),
                dma((nu * ni,)), dma(()), dma((nu * ni,)), dma(()),
            ],
            compiler_params=pltpu.CompilerParams(collective_id=0, has_side_effects=True),
        )(inv, item_factors, item_gram, tile_values.reshape(slots, side, side))
        sol, item = pl.pallas_call(
            place_outputs,
            out_shape=(
                jax.ShapeDtypeStruct((rows, rank), f4),
                jax.ShapeDtypeStruct((cols, rank), f4),
            ),
            in_specs=[vmem, vmem],
            out_specs=(vmem, vmem),
        )(sol, item)
        return sol, item[None]

    return local


def solution(mesh):
    return jax.shard_map(
        make_local(mesh.shape["user"], mesh.shape["item"]),
        mesh=mesh,
        in_specs=(
            P("item", None),
            P(),
            P("user", "item", None),
            P("user", "item", None),
            P("user", "item"),
            P("user", "item", None, None, None),
        ),
        out_specs=(P(("user", "item"), None), P("item", "user", None)),
        check_vma=False,
    )
```

time: 65.5 us -> 63.7 us (0.973)
  Pallas kernels: 62.7 us -> 60.9 us
    pallas_call x1, Pallas kernels: 60.8 us -> 59 us  [local(): pl.pallas_call(functools.partial(kernel, nu, ni, scale), out_shape=(jax.S...]
    reduce_sum x1, other arithmetic: 0.1 us -> 1.29 us  [local(): inv = jnp.sum(jnp.where(match, slots - at[None, :], 0), axis=1)]
    select_n x1, other arithmetic: 0.68 us -> 0.01 us  [local(): cell % blocks]
where the time goes in v1:
time: 63.7 us; the launch traced here: 63.5 us
  Pallas kernels  60.9 us (96%)
  other arithmetic  1.3 us (2%)
  between operations  1.3 us (2%)
    pallas_call x1, Pallas kernels, local(): pl.pallas_call(functools.partial(kernel, nu, ni, scale), out_shape=(jax.S...  59 us
    pallas_call x1, Pallas kernels, local(): pl.pallas_call(place_outputs, out_shape=(jax.ShapeDtypeStruct((rows, rank...  1.91 us
    reduce_sum x1, other arithmetic, local(): inv = jnp.sum(jnp.where(match, slots - at[None, :], 0), axis=1)  1.29 us

profile of v1, /device:TPU:0, one launch (start us, length us, event | category | flops | bytes accessed | tf_op | source)
XLA Modules:
  0.0 63.5 jit_solution(9188253780441289829)
XLA Ops:
  1.3 1.3 %select_reduce_fusion.inv_ref = s32[64]{0:T(128)} fusion(s32[48]{0:T(128)S(1)} %iota_subtract_fusion, s32[64]{0:T(128)S(1)} %get-tuple-element.10, s32[64]{0:T(128)S(1)} %get-tuple-element.11, s32[48]{0:T(128)} %bitcast.7, s32[48]{0:T(128)} %bitcast.8, pred[48]{0:T(512)(128)(4,1)S(1)} %iota_compare_fusion), kind=kLoop, calls=%fused_computation | loop fusion | flops 18368 | bytes 1392 | tf_op jit(solution)/shard_map/reduce_sum | solution.py:486
  2.6 59.0 %shard_map.77 = (f32[64,256]{1,0:T(8,128)}, f32[512,256]{1,0:T(8,128)}) custom-call(s32[64]{0:T(128)} %select_reduce_fusion.inv_ref, bf16[2048,256]{1,0:T(8,128)(2,1)} %y_hbm.1, f32[256,256]{1,0:T(8,128)} %gram_hbm.1, bf16[48,128,128]{2,1,0:T(8,128)(2,1)} %bitcast.6), custom_call_target="tpu_custom_call" | custom-call | tf_op jit(solution)/shard_map/pallas_call | solution.py:494
  61.6 1.9 %shard_map.78 = (f32[64,256]{1,0:T(8,128)}, f32[512,256]{1,0:T(8,128)}) custom-call(f32[64,256]{1,0:T(8,128)} %get-tuple-element.6.sol_in, f32[512,256]{1,0:T(8,128)} %get-tuple-element.7.item_in), custom_call_target="tpu_custom_call" | custom-call | tf_op jit(solution)/shard_map/pallas_call | solution.py:541
  (3 shorter events, 0.0 us)

commit v2 on v1

--- a/solution.py
+++ b/solution.py
@@ -1,4 +1,5 @@
 import functools
+import math
 
 import jax
 import jax.numpy as jnp
@@ -29,12 +30,12 @@
     nu, ni, scale,
     inv_ref, y_hbm, gram_hbm, tiles_hbm,
     sol_ref, item_ref,
-    tiles, yv, gram, wide, ws, wx, ct, xb, pa, ra, own, sb, rb,
+    tiles, yv, gram, wide, ws, turned, ct, xb, pa, ra, own, sb, rb,
     d_state, r_state, x_state, n_state, i_state, a_state, sol_in,
-    scal, sums, coef, x2,
+    scal, sums, coef, x2, kept, outgo, income,
     load_sem, w_send, w_recv, a_send, a_recv, y_send, y_recv, b_send, b_recv,
-    z_send, z_recv, f_send, f_recv, u_send, u_recv, s_send, s_recv, o_send, o_recv,
-    c_send, c_recv, p_send, p_recv,
+    z_send, z_recv, f_send, f_recv, u_send, u_recv, o_send, o_recv,
+    c_send, c_recv, p_send, p_recv, r_send, r_recv,
 ):
     slots, side, _ = tiles_hbm.shape
     items, rank = y_hbm.shape
@@ -52,19 +53,30 @@
     g, o = lax.axis_index("user"), lax.axis_index("item")
     z, c = lax.div(o, 2), lax.rem(o, 2)
     other = 1 - c
-    me = g * ni + o
     sib = {"item": z * 2 + other}
     place = lax.rem(z - low + nz, owners)
     is_owner = (z >= low) & (z < low + owners)
 
-    def unum(j):
-        return lax.rem(g + (j + nu), nu)
+    line = math.isqrt(nu)
+    assert line * line == nu
+    gx, gy = lax.rem(g, line), lax.div(g, line)
+
+    def grid(x, y):
+        return lax.rem(x, line) + line * lax.rem(y, line)
+
+    def unum(i, j):
+        return jnp.where(c == 0, grid(gx + i, gy + j), grid(gx + j, gy + i))
+
+    def far(j, size):
+        return min(j, size - j)
+
+    zothers = sorted(range(1, nz), key=lambda j: -far(j, nz))
 
     def zpeer(j):
         return {"item": lax.rem(z + (j + nz), nz) * 2 + c}
 
-    def upeer(j):
-        return {"user": unum(j)}
+    def upeer(i, j=0):
+        return {"user": unum(i, j)}
 
     def peer(i):
         return {"user": lax.rem(g + lax.div(i, ni), nu), "item": lax.rem(o + lax.rem(i, ni), ni)}
@@ -130,21 +142,11 @@
     def wcol(gg):
         return pl.ds(pl.multiple_of(gg * cols, cols), cols)
 
-    def turn(j):
-        if j == 0:
-            block = wide[:, wcol(g)]
-        else:
-            arrived(wx.at[j], w_send.at[j], w_recv.at[j], upeer(-j))
-            block = wx[j]
-        ct[j] = confidence_of(block).T
-
-    turns = [[], [], [], []]
-    for j in range(nu):
-        turns[j * 4 // nu].append(j)
-
-    def turn_all(which):
-        for j in turns[which]:
-            turn(j)
+    def turn(i, j):
+        to = ct.at[0, j] if i == 0 else turned.at[i - 1, j]
+        to[...] = confidence_of(wide[:, wcol(unum(i, j))]).T
+        if i:
+            rcopy(to, ct.at[i, j], w_send, w_recv, upeer(i)).start()
 
     def rhs_pass(hh):
         here = slice(hh * half, (hh + 1) * half)
@@ -182,30 +184,40 @@
                     acc = acc + prod[:, j * LANES : (j + 1) * LANES]
         for q in range(owners):
             mine = [acc[(s * owners + q) * rows : (s * owners + q + 1) * rows] for s in range(STREAMS)]
-            sums[me, q : q + 1, 0:per] = jnp.sum(jnp.concatenate(mine, axis=0).T, axis=0, keepdims=True)
+            sums[o, q : q + 1, 0:per] = jnp.sum(jnp.concatenate(mine, axis=0).T, axis=0, keepdims=True)
 
     def reduce_start(k, s, total):
         own[s] = total
         sb[k, s] = total.astype(jnp.bfloat16)
-        for q in range(owners):
+        for i in range(owners):
+            q = jnp.where(z * 2 < nz, owners - 1 - i, i)
             zo = q + low
             j = lax.rem(zo - z + nz, nz)
-            part = sb.at[k, s, pl.ds(q * rows, rows)]
-            send_if(
-                z != zo, part, rb.at[k, s, j], b_send.at[k, s, q], b_recv.at[k, s, j], {"item": zo * 2 + c}
-            )
+            part = sb.at[k, s, pl.ds(pl.multiple_of(q * rows, rows), rows)]
+            cp = rcopy(part, rb.at[k, s, j], b_send.at[s, i], b_recv.at[s], {"item": zo * 2 + c})
+            pl.when(z != zo)(cp.start)
+
+    def reduce_sent(k, s):
+        for i in range(owners):
+            zo = jnp.where(z * 2 < nz, owners - 1 - i, i) + low
+            part = sb.at[k, s, pl.ds(0, rows)]
+            pl.when(z != zo)(rcopy(part, part, b_send.at[s, i], b_recv.at[s], sib).wait_send)
 
     def reduce_end(k, s):
         total = own[s, pl.ds(pl.multiple_of(place * rows, rows), rows), :]
+        arrived(rb.at[k, s, pl.ds(1, nz - 1)], b_send.at[s, 0], b_recv.at[s], sib)
         for j in range(1, nz):
-            arrived(rb.at[k, s, j], b_send.at[k, s, 0], b_recv.at[k, s, j], zpeer(-j))
             total = total + rb[k, s, j].astype(jnp.float32)
         return total
 
     def gather_send(k, s):
         mine = xb.at[k, 0, piece(s, place)]
-        for j in range(1, nz):
-            send_if(is_owner, mine, mine, z_send.at[k, s, j], z_recv.at[k, s, place], zpeer(j))
+        for j in zothers:
+            rcopy(mine, mine, z_send.at[s], z_recv.at[s, place], zpeer(j)).start()
+
+    def gather_sent(k, s):
+        every = rb.at[k, s, pl.ds(1, nz - 1)]
+        rcopy(every, every, z_send.at[s], z_recv.at[s, 0], sib).wait_send()
 
     def gather_end(k, s, pass_on):
         for q in range(owners):
@@ -214,31 +226,32 @@
 
             @pl.when(z != zo)
             def _():
-                arrived(got, z_send.at[k, s, 0], z_recv.at[k, s, q], {"item": lax.rem(o + 2, ni)})
+                arrived(got, z_send.at[s], z_recv.at[s, q], sib)
 
             if pass_on:
-                for v in range(1, nu):
-                    send(got, xb.at[k, v, piece(s, q)], u_send.at[k, v, s, q], u_recv.at[k, v, s, q], upeer(v))
-                send(got, xb.at[k, 0, piece(s, q, 1)], f_send.at[k, s, q], f_recv.at[k, s, q], sib)
+                rcopy(got, xb.at[k, 0, piece(s, q, 1)], f_send.at[k], f_recv.at[k], sib).start()
+                for i in range(1, line):
+                    rcopy(got, xb.at[k, i, piece(s, q)], u_send.at[k], u_recv.at[k], upeer(i)).start()
 
     mine_all, theirs_all = pl.ds(0, half), pl.ds(half, half)
+    away = pl.ds(1, line - 1)
 
     def basis_send(k):
         mine = xb.at[k, 0, mine_all]
-        for v in range(1, nu):
-            send(mine, xb.at[k, v, mine_all], u_send.at[k, v, 0, 0], u_recv.at[k, v, 0, 0], upeer(v))
-        send(mine, xb.at[k, 0, theirs_all], f_send.at[k, 0, 0], f_recv.at[k, 0, 0], sib)
-
-    def basis_pass(k):
-        for v in range(1, nu):
-            got = xb.at[k, v, mine_all]
-            arrived(got, u_send.at[k, v, 0, 0], u_recv.at[k, v, 0, 0], upeer(-v))
-            send(got, xb.at[k, v, theirs_all], s_send.at[k, v, 0, 0], s_recv.at[k, v, 0, 0], sib)
+        rcopy(mine, xb.at[k, 0, theirs_all], f_send.at[k], f_recv.at[k], sib).start()
+
+    def basis_pass(k, which=slice(None)):
+        arrived(xb.at[k, 0, theirs_all], f_send.at[k], f_recv.at[k], sib)
+        for i in range(1, line):
+            rcopy(xb.at[k, 0, which], xb.at[k, i, which], u_send.at[k], u_recv.at[k], upeer(i)).start()
 
     def basis_end(k):
-        arrived(xb.at[k, 0, theirs_all], f_send.at[k, 0, 0], f_recv.at[k, 0, 0], sib)
-        for v in range(1, nu):
-            arrived(xb.at[k, v, theirs_all], s_send.at[k, v, 0, 0], s_recv.at[k, v, 0, 0], sib)
+        arrived(xb.at[k, away], u_send.at[k], u_recv.at[k], sib)
+
+    def basis_sent(k):
+        mine, got = xb.at[k, 0, mine_all], xb.at[k, away]
+        rcopy(mine, mine, f_send.at[k], f_recv.at[k], sib).wait_send()
+        rcopy(got, got, u_send.at[k], u_recv.at[k], sib).wait_send()
 
     def update(k, s):
         total = reduce_end(k, s)
@@ -269,21 +282,34 @@
                 d_state[s], gram[...], precision=highest, preferred_element_type=jnp.float32
             )
 
-    def spread(src, ss, rs):
-        def body(i, carry):
-            rcopy(src, src, ss.at[i], rs, peer(i)).start()
+    def spread(slot, ss, near, far_off):
+        def column(t, carry):
+            dev = {"item": lax.rem(o + t, ni)}
+            rcopy(slot(0), slot(0), ss, near, dev).start()
             return carry
 
-        lax.fori_loop(1, devices, body, 0)
-
-    def spread_end(src, ss, rs):
-        def body(i, carry):
-            rcopy(src, src, ss.at[i], rs, peer(i)).wait_send()
-            return carry
-
-        lax.fori_loop(1, devices, body, 0)
-
-    my_scal = scal.at[(g * owners + place) * 2 + c]
+        lax.fori_loop(1, ni, column, 0)
+        for e in range(2):
+            for t in range(1, line):
+                gg = grid(gx + t, gy) if e == 0 else grid(gx, gy + t)
+
+                def across(zz, carry):
+                    dev = {"user": gg, "item": lax.rem(z + zz, nz) * 2 + e}
+                    rcopy(slot(0), slot(t), ss, far_off, dev).start()
+                    return carry
+
+                lax.fori_loop(0, nz, across, 0)
+
+    def spread_end(every, ss, rs):
+        rcopy(every, every, ss, rs, sib).wait_send()
+
+    told = (ni - 1) + 2 * (line - 1) * nz
+
+    def scal_slot(t):
+        return scal.at[(t * owners + place) * 2 + c]
+
+    def sums_slot(t):
+        return sums.at[(t * nz + z) * 2 + c]
 
     def tell():
         grams()
@@ -294,45 +320,46 @@
             at = jnp.where(lane == 2, n_state[s], turned)
             at = jnp.where(lane == 1, a_state[1, s], at)
             parts.append(jnp.where(lane == 0, a_state[0, s], at))
-        my_scal[:, 0:per] = jnp.concatenate(parts, axis=0).T[0:8]
-        spread(my_scal, c_send, c_recv)
+        scal[place * 2 + c, :, 0:per] = jnp.concatenate(parts, axis=0).T[0:8]
+        spread(scal_slot, c_send, c_recv, c_recv)
+
+    def step(k, s):
+        update(k, s)
+        gather_send(k, s)
 
     pa[...] = rhs_pass(1)
     pl.semaphore_wait(barrier, devices - 1)
-    for s in range(STREAMS):
-        here = pl.ds(s * srows, srows)
-        send(pa.at[here], ra.at[here], a_send.at[s], a_recv.at[s], sib)
+    send(pa, ra, a_send, a_recv, sib)
     first = rhs_pass(0)
     for s in range(STREAMS):
         own[s] = first[s * srows : (s + 1) * srows]
     send(yv.at[0], yv.at[1], y_send.at[0], y_recv.at[0], sib)
     send(wide.at[theirs_all], ws, y_send.at[1], y_recv.at[1], sib)
+    arrived(ra, a_send, a_recv, sib)
     for s in range(STREAMS):
-        here = pl.ds(s * srows, srows)
-        arrived(ra.at[here], a_send.at[s], a_recv.at[s], sib)
-        reduce_start(0, s, own[s] + ra[here, :])
-    for j in range(1, nu):
-        send(wide.at[:, wcol(unum(j))], wx.at[j], w_send.at[j], w_recv.at[j], upeer(j))
-    turn_all(0)
+        reduce_start(0, s, own[s] + ra[s * srows : (s + 1) * srows, :])
+    for i in range(1, line):
+        for j in range(line):
+            turn(i, j)
     for s in range(STREAMS):
-        pl.when(is_owner)(functools.partial(update, 0, s))
-        gather_send(0, s)
+        pl.when(is_owner)(functools.partial(step, 0, s))
+    for j in range(line):
+        turn(0, j)
     arrived(yv.at[1], y_send.at[0], y_recv.at[0], sib)
     arrived(ws, y_send.at[1], y_recv.at[1], sib)
 
     for k in range(1, ITERS):
         for s in range(STREAMS):
             gather_end(k - 1, s, False)
-            reduce_start(k, s, stream_pass(k, s))
+            total = stream_pass(k, s)
+            reduce_sent(k - 1, s)
+            reduce_start(k, s, total)
         basis_send(k - 1)
         pl.when(is_owner)(grams)
-        if k == 1:
-            turn_all(1)
-        if k == 2:
-            basis_pass(0)
         for s in range(STREAMS):
-            pl.when(is_owner)(functools.partial(update, k, s))
-            gather_send(k, s)
+            pl.when(is_owner)(functools.partial(gather_sent, k - 1, s))
+            pl.when(is_owner)(functools.partial(step, k, s))
+        basis_pass(k - 1)
 
     pl.when(is_owner)(tell)
     for q in range(owners):
@@ -346,42 +373,40 @@
     for s in range(STREAMS):
         gather_end(k, s, True)
     last_pass()
-    spread(sums.at[me], p_send, p_recv)
-
-    basis_pass(1)
-    turn_all(2)
-    turn_all(3)
-    known = scal.shape[0]
+    spread(sums_slot, p_send, p_recv.at[0], p_recv.at[1])
+    basis_pass(k, theirs_all)
+    known = line * owners * 2
 
     @pl.when(is_owner)
     def _():
-        every = scal.at[pl.ds(0, known - 1)]
-        arrived(every, c_send.at[0], c_recv, sib)
+        arrived(scal.at[pl.ds(0, known - 1)], c_send, c_recv, sib)
 
     @pl.when(jnp.logical_not(is_owner))
     def _():
-        arrived(scal, c_send.at[0], c_recv, sib)
+        arrived(scal.at[pl.ds(0, known)], c_send, c_recv, sib)
 
     def cell(v, hh, q):
         return (v * 2 + hh) * owners + q
 
-    def cells():
-        for v in range(nu):
+    def cells(groups):
+        for v in groups:
             for hh in range(2):
                 for q in range(owners):
-                    yield v, hh, q, unum(-v), (c if hh == 0 else other)
+                    yield v, hh, q, (c if hh == 0 else other)
+
+    every = range(line)
 
     def block(v, hh, s, q):
         at = ((hh * STREAMS + s) * owners + q) * rows
         return slice(at, at + rows)
 
-    for v, hh, q, gv, cc in cells():
+    for v, hh, q, cc in cells(every):
         n = cell(v, hh, q)
-        coef[0:4, n, :] = scal[(gv * owners + q) * 2 + cc][0:4]
+        coef[0:4, n, :] = scal[(v * owners + q) * 2 + cc][0:4]
     alpha1, alpha2 = coef[0].T, coef[1].T
-    for j in range(2):
+    for j in range(k):
         basis_end(j)
-    for v, hh, q, gv, cc in cells():
+    for v, hh, q, cc in cells(every):
         n = cell(v, hh, q)
         for s in range(STREAMS):
             at = block(v, hh, s, q)
@@ -390,21 +415,33 @@
                 r, n : n + 1
             ] * xb[1, v, at, :].astype(jnp.float32)
 
-    for v in range(1, nu):
-        for s in range(STREAMS):
-            for q in range(owners):
-                got = xb.at[k, v, piece(s, q)]
-                arrived(got, u_send.at[k, v, s, q], u_recv.at[k, v, s, q], upeer(-v))
-                send(got, xb.at[k, v, piece(s, q, 1)], s_send.at[k, v, s, q], s_recv.at[k, v, s, q], sib)
-
-    arrived(sums.at[pl.ds(0, devices - 1)], p_send.at[0], p_recv, sib)
-    for v, hh, q, gv, cc in cells():
-        n = cell(v, hh, q)
-        total = coef[3, n : n + 1, :]
-        for zz in range(nz):
-            total = total + sums[gv * ni + zz * 2 + cc, q : q + 1, :]
-        coef[4, n : n + 1, :] = coef[2, n : n + 1, :] / (total + epsilon)
-    alpha3 = coef[4].T
+    def alphas(groups):
+        for v, hh, q, cc in cells(groups):
+            n = cell(v, hh, q)
+            total = coef[3, n : n + 1, :]
+            for zz in range(nz):
+                total = total + sums[(v * nz + zz) * 2 + cc, q : q + 1, :]
+            coef[4, n : n + 1, :] = coef[2, n : n + 1, :] / (total + epsilon)
+        return coef[4].T
+
+    def final_of(v, alpha):
+        parts = []
+        for hh in range(2):
+            for s in range(STREAMS):
+                for q in range(owners):
+                    n = cell(v, hh, q)
+                    at = block(v, hh, s, q)
+                    parts.append(
+                        x2[v, at, :]
+                        + alpha[s * rows : (s + 1) * rows, n : n + 1] * xb[k, v, at, :].astype(jnp.float32)
+                    )
+        return jnp.concatenate(parts, axis=0).astype(jnp.bfloat16)
+
+    arrived(sums.at[pl.ds(0, ni - 1)], p_send, p_recv.at[0], sib)
+    alpha3 = alphas([0])
+    final = final_of(0, alpha3)
+    for j in range(line):
+        kept[j] = jnp.dot(ct[0, j], final, preferred_element_type=jnp.float32)
 
     for target in range(nz):
         owner = target // STREAMS + low
@@ -422,43 +459,40 @@
                 k, 0, block(0, 0, s, q), :
             ].astype(jnp.float32)
 
-    for v in range(nu):
-        total = None
-        for hh in range(2):
-            parts = []
-            for s in range(STREAMS):
-                for q in range(owners):
-                    if hh == 1:
-                        got = xb.at[k, v, piece(s, q, 1)]
-                        if v:
-                            arrived(got, s_send.at[k, v, s, q], s_recv.at[k, v, s, q], sib)
-                        else:
-                            arrived(got, f_send.at[k, s, q], f_recv.at[k, s, q], sib)
-                    n = cell(v, hh, q)
-                    at = block(v, hh, s, q)
-                    parts.append(
-                        x2[v, at, :]
-                        + alpha3[s * rows : (s + 1) * rows, n : n + 1] * xb[k, v, at, :].astype(jnp.float32)
-                    )
-            final = jnp.concatenate(parts, axis=0).astype(jnp.bfloat16)
-            term = jnp.dot(
-                ct[v, :, hh * half : (hh + 1) * half], final, preferred_element_type=jnp.float32
-            )
-            total = term if total is None else total + term
-        if v == 0:
+    arrived(sums.at[pl.ds(0, (line - 1) * ni)], p_send, p_recv.at[1], sib)
+    alpha3 = alphas(range(1, line))
+    arrived(ct.at[away], w_send, w_recv, sib)
+    basis_end(k)
+    finals = [final_of(v, alpha3) for v in range(1, line)]
+    for j in list(range(1, line)) + [0]:
+        total = kept[j]
+        for v in range(1, line):
+            total = total + jnp.dot(ct[v, j], finals[v - 1], preferred_element_type=jnp.float32)
+        if j:
+            outgo[j - 1] = total.astype(jnp.bfloat16)
+            rcopy(outgo.at[j - 1], income.at[j - 1], r_send, r_recv, upeer(0, j)).start()
+        else:
             item_ref[...] = total
-        elif v < nu - 1:
-            item_ref[...] += total
-        else:
-            item_ref[...] = (item_ref[...] + total) * scale
+    arrived(income, r_send, r_recv, sib)
+    total = item_ref[...]
+    for j in range(line - 1):
+        total = total + income[j].astype(jnp.float32)
+    item_ref[...] = total * scale
 
     for cond, cp in sent:
         if cond is None:
             cp.wait_send()
         else:
             pl.when(cond)(cp.wait_send)
-    spread_end(sums.at[me], p_send, p_recv)
-    pl.when(is_owner)(functools.partial(spread_end, my_scal, c_send, c_recv))
+    for j in range(ITERS):
+        basis_sent(j)
+    for s in range(STREAMS):
+        reduce_sent(k, s)
+        pl.when(is_owner)(functools.partial(gather_sent, k, s))
+    rcopy(turned, turned, w_send, w_recv, sib).wait_send()
+    spread_end(sums.at[pl.ds(0, told)], p_send, p_recv.at[0])
+    pl.when(is_owner)(functools.partial(spread_end, scal.at[pl.ds(0, told)], c_send, c_recv))
+    rcopy(outgo, outgo, r_send, r_recv, sib).wait_send()
 
 
 def place_outputs(sol_in, item_in, sol_out, item_out):
@@ -488,7 +522,8 @@
         bf, f4 = jnp.bfloat16, jnp.float32
         dma = pltpu.SemaphoreType.DMA
         vm = pltpu.VMEM
-        cells = max(8, nu * 2 * owners)
+        line = math.isqrt(nu)
+        cells = max(8, line * 2 * owners)
         anywhere = pl.BlockSpec(memory_space=pl.ANY)
         vmem = pl.BlockSpec(memory_space=pltpu.VMEM)
         sol, item = pl.pallas_call(
@@ -505,9 +540,9 @@
                 vm((rank, rank), f4),
                 vm((group, items), bf),
                 vm((half, items), bf),
-                vm((nu, group, cols), bf),
-                vm((nu, cols, group), bf),
-                vm((ITERS, nu, group, rank), bf),
+                vm((line - 1, line, cols, group), bf),
+                vm((line, line, cols, group), bf),
+                vm((ITERS, line, group, rank), bf),
                 vm((half, rank), f4),
                 vm((half, rank), f4),
                 vm((STREAMS, srows, rank), f4),
@@ -520,21 +555,24 @@
                 vm((STREAMS, rows, rank), f4),
                 vm((2, STREAMS, rows, 1), f4),
                 vm((rows, rank), f4),
-                vm((nu * owners * 2, 8, LANES), f4),
-                vm((nu * ni, owners, LANES), f4),
+                vm((line * ni, 8, LANES), f4),
+                vm((line * ni, owners, LANES), f4),
                 vm((5, cells, LANES), f4),
-                vm((nu, group, rank), f4),
+                vm((line, group, rank), f4),
+                vm((line, cols, rank), f4),
+                vm((line - 1, cols, rank), bf),
+                vm((line - 1, cols, rank), bf),
                 dma((3,)),
-                dma((nu,)), dma((nu,)),
-                dma((STREAMS,)), dma((STREAMS,)),
+                dma(()), dma(()),
+                dma(()), dma(()),
                 dma((2,)), dma((2,)),
-                dma((ITERS, STREAMS, owners)), dma((ITERS, STREAMS, nz)),
-                dma((ITERS, STREAMS, nz)), dma((ITERS, STREAMS, owners)),
-                dma((ITERS, STREAMS, owners)), dma((ITERS, STREAMS, owners)),
-                dma((ITERS, nu, STREAMS, owners)), dma((ITERS, nu, STREAMS, owners)),
-                dma((ITERS, nu, STREAMS, owners)), dma((ITERS, nu, STREAMS, owners)),
+                dma((STREAMS, owners)), dma((STREAMS,)),
+                dma((STREAMS,)), dma((STREAMS, owners)),
+                dma((ITERS,)), dma((ITERS,)),
+                dma((ITERS,)), dma((ITERS,)),
                 dma((STREAMS,)), dma(()),
-                dma((nu * ni,)), dma(()), dma((nu * ni,)), dma(()),
+                dma(()), dma(()), dma(()), dma((2,)),
+                dma(()), dma(()),
             ],
             compiler_params=pltpu.CompilerParams(collective_id=0, has_side_effects=True),
         )(inv, item_factors, item_gram, tile_values.reshape(slots, side, side))

time: 63.7 us -> 52.5 us (0.82)
  Pallas kernels: 60.9 us -> 49.7 us
    pallas_call x1, Pallas kernels: 59 us -> 47.8 us  [local(): pl.pallas_call(functools.partial(kernel, nu, ni, scale), out_shape=(jax.S...]
where the time goes in v2:
time: 52.5 us; the launch traced here: 52.3 us
  Pallas kernels  49.7 us (95%)
  other arithmetic  1.3 us (2%)
  between operations  1.3 us (2%)
    pallas_call x1, Pallas kernels, local(): pl.pallas_call(functools.partial(kernel, nu, ni, scale), out_shape=(jax.S...  47.8 us
    pallas_call x1, Pallas kernels, local(): pl.pallas_call(place_outputs, out_shape=(jax.ShapeDtypeStruct((rows, rank...  1.91 us
    reduce_sum x1, other arithmetic, local(): inv = jnp.sum(jnp.where(match, slots - at[None, :], 0), axis=1)  1.29 us

profile of v2, /device:TPU:0, one launch (start us, length us, event | category | flops | bytes accessed | tf_op | source)
XLA Modules:
  0.0 52.3 jit_solution(8215236221728744584)
XLA Ops:
  1.3 1.3 %select_reduce_fusion.inv_ref = s32[64]{0:T(128)} fusion(s32[48]{0:T(128)S(1)} %iota_subtract_fusion, s32[64]{0:T(128)S(1)} %get-tuple-element.10, s32[64]{0:T(128)S(1)} %get-tuple-element.11, s32[48]{0:T(128)} %bitcast.7, s32[48]{0:T(128)} %bitcast.8, pred[48]{0:T(512)(128)(4,1)S(1)} %iota_compare_fusion), kind=kLoop, calls=%fused_computation | loop fusion | flops 18368 | bytes 1392 | tf_op jit(solution)/shard_map/reduce_sum | solution.py:520
  2.6 47.8 %shard_map.77 = (f32[64,256]{1,0:T(8,128)}, f32[512,256]{1,0:T(8,128)}) custom-call(s32[64]{0:T(128)} %select_reduce_fusion.inv_ref, bf16[2048,256]{1,0:T(8,128)(2,1)} %y_hbm.1, f32[256,256]{1,0:T(8,128)} %gram_hbm.1, bf16[48,128,128]{2,1,0:T(8,128)(2,1)} %bitcast.6), custom_call_target="tpu_custom_call" | custom-call | tf_op jit(solution)/shard_map/pallas_call | solution.py:529
  50.4 1.9 %shard_map.78 = (f32[64,256]{1,0:T(8,128)}, f32[512,256]{1,0:T(8,128)}) custom-call(f32[64,256]{1,0:T(8,128)} %get-tuple-element.6.sol_in, f32[512,256]{1,0:T(8,128)} %get-tuple-element.7.item_in), custom_call_target="tpu_custom_call" | custom-call | tf_op jit(solution)/shard_map/pallas_call | solution.py:579
  (3 shorter events, 0.0 us)

commit v3 on v2

--- a/solution.py
+++ b/solution.py
@@ -28,9 +28,9 @@
 
 def kernel(
     nu, ni, scale,
-    inv_ref, y_hbm, gram_hbm, tiles_hbm,
+    users_hbm, items_hbm, counts_hbm, y_hbm, gram_hbm, tiles_hbm,
     sol_ref, item_ref,
-    tiles, yv, gram, wide, ws, turned, ct, xb, pa, ra, own, sb, rb,
+    users_in, items_in, count_in, slot_of, inv_ref, tiles, yv, gram, wide, ws, turned, ct, xb, pa, ra, own, sb, rb,
     d_state, r_state, x_state, n_state, i_state, a_state, sol_in,
     scal, sums, coef, x2, kept, outgo, income,
     load_sem, w_send, w_recv, a_send, a_recv, y_send, y_recv, b_send, b_recv,
@@ -112,7 +112,12 @@
         pltpu.make_async_copy(y_hbm, yv.at[0], load_sem.at[1]),
         pltpu.make_async_copy(gram_hbm, gram, load_sem.at[2]),
     ]
-    for cp in loads:
+    index = [
+        pltpu.make_async_copy(users_hbm, users_in, load_sem.at[3]),
+        pltpu.make_async_copy(items_hbm, items_in, load_sem.at[4]),
+        pltpu.make_async_copy(counts_hbm, count_in, load_sem.at[5]),
+    ]
+    for cp in index + loads:
         cp.start()
 
     barrier = pltpu.get_barrier_semaphore()
@@ -124,6 +129,16 @@
     lax.fori_loop(1, devices, greet, 0)
 
     tiles[slots] = jnp.zeros((side, side), jnp.bfloat16)
+    for cp in index:
+        cp.wait()
+    lane = lax.broadcasted_iota(jnp.int32, (1, slots), 1)
+    key = jnp.where(lane < count_in[...], users_in[0] * blocks + items_in[0], -1)
+    match = lax.broadcasted_iota(jnp.int32, (LANES, slots), 0) == key
+    found = jnp.min(jnp.where(match, lane, slots), axis=1, keepdims=True)
+    slot_of[...] = jnp.broadcast_to(found, (LANES, LANES)).T[0:8]
+    to_scalar = pltpu.make_async_copy(slot_of, inv_ref, load_sem.at[6])
+    to_scalar.start()
+    to_scalar.wait()
     loads[0].wait()
     for b in range(blocks):
         for q in range(owners):
@@ -134,7 +149,7 @@
                     to = ((hh * STREAMS + s) * owners + q) * rows
                     at = pl.ds(pl.multiple_of(off + (c if hh == 0 else other) * rows, rows), rows)
                     wide[to : to + rows, b * side : (b + 1) * side] = tiles[
-                        slots - inv_ref[u * blocks + b], at, :
+                        inv_ref[0, u * blocks + b], at, :
                     ]
     for cp in loads[1:]:
         cp.wait()
@@ -495,9 +510,15 @@
     rcopy(outgo, outgo, r_send, r_recv, sib).wait_send()
 
 
-def place_outputs(sol_in, item_in, sol_out, item_out):
-    sol_out[...] = sol_in[...]
-    item_out[...] = item_in[...]
+def place_outputs(sol_in, item_in, sol_out, item_out, sem):
+    copies = [
+        pltpu.make_async_copy(item_in, item_out, sem.at[0]),
+        pltpu.make_async_copy(sol_in, sol_out, sem.at[1]),
+    ]
+    for cp in copies:
+        cp.start()
+    for cp in copies:
+        cp.wait()
 
 
 def make_local(nu, ni):
@@ -512,12 +533,6 @@
         owners = nz // STREAMS
         srows = owners * rows
         cols = items // nu
-        at = jnp.arange(slots, dtype=jnp.int32)
-        cell = jnp.arange(USER_BLK * blocks, dtype=jnp.int32)[:, None]
-        match = (
-            (tile_users[0] == cell // blocks) & (tile_items[0] == cell % blocks) & (at[None, :] < tile_counts[0, 0])
-        )
-        inv = jnp.sum(jnp.where(match, slots - at[None, :], 0), axis=1)
         scale = float(nu * group) ** -0.5
         bf, f4 = jnp.bfloat16, jnp.float32
         dma = pltpu.SemaphoreType.DMA
@@ -528,13 +543,15 @@
         vmem = pl.BlockSpec(memory_space=pltpu.VMEM)
         sol, item = pl.pallas_call(
             functools.partial(kernel, nu, ni, scale),
-            out_shape=(
-                jax.ShapeDtypeStruct((rows, rank), f4),
-                jax.ShapeDtypeStruct((cols, rank), f4),
-            ),
-            in_specs=[pl.BlockSpec(memory_space=pltpu.SMEM), anywhere, anywhere, anywhere],
+            out_shape=(vm((rows, rank), f4), vm((cols, rank), f4)),
+            in_specs=[anywhere] * 6,
             out_specs=(vmem, vmem),
             scratch_shapes=[
+                vm((1, 1, slots), jnp.int32),
+                vm((1, 1, slots), jnp.int32),
+                vm((1, 1), jnp.int32),
+                vm((8, LANES), jnp.int32),
+                pltpu.SMEM((8, LANES), jnp.int32),
                 vm((slots + 1, side, side), bf),
                 vm((2, items, rank), bf),
                 vm((rank, rank), f4),
@@ -562,7 +579,7 @@
                 vm((line, cols, rank), f4),
                 vm((line - 1, cols, rank), bf),
                 vm((line - 1, cols, rank), bf),
-                dma((3,)),
+                dma((7,)),
                 dma(()), dma(()),
                 dma(()), dma(()),
                 dma((2,)), dma((2,)),
@@ -575,7 +592,9 @@
                 dma(()), dma(()),
             ],
             compiler_params=pltpu.CompilerParams(collective_id=0, has_side_effects=True),
-        )(inv, item_factors, item_gram, tile_values.reshape(slots, side, side))
+        )(tile_users, tile_items, tile_counts, item_factors, item_gram, tile_values.reshape(slots, side, side))
+        sol = pltpu.with_memory_space_constraint(sol, pltpu.VMEM)
+        item = pltpu.with_memory_space_constraint(item, pltpu.VMEM)
         sol, item = pl.pallas_call(
             place_outputs,
             out_shape=(
@@ -583,7 +602,8 @@
                 jax.ShapeDtypeStruct((cols, rank), f4),
             ),
             in_specs=[vmem, vmem],
-            out_specs=(vmem, vmem),
+            out_specs=(anywhere, anywhere),
+            scratch_shapes=[dma((2,))],
         )(sol, item)
         return sol, item[None]
 

time: 52.5 us -> 48.7 us (0.928)
  Pallas kernels: 49.7 us -> 47.2 us
  other arithmetic: 1.3 us -> 0 us
    pallas_call x1, Pallas kernels: 47.8 us -> 46.4 us  [local(): pl.pallas_call(functools.partial(kernel, nu, ni, scale), out_shape=(vm((r...]
    reduce_sum x1 -> x0, other arithmetic: 1.29 us -> none  [local(): inv = jnp.sum(jnp.where(match, slots - at[None, :], 0), axis=1)]
    pallas_call x1, Pallas kernels: 1.91 us -> 0.82 us  [local(): pl.pallas_call(place_outputs, out_shape=(jax.ShapeDtypeStruct((rows, rank...]
where the time goes in v3:
time: 48.7 us; the launch traced here: 48.5 us
  Pallas kernels  47.2 us (97%)
  between operations  1.29 us (3%)
    pallas_call x1, Pallas kernels, local(): pl.pallas_call(functools.partial(kernel, nu, ni, scale), out_shape=(vm((r...  46.4 us

profile of v3, /device:TPU:0, one launch (start us, length us, event | category | flops | bytes accessed | tf_op | source)
XLA Modules:
  0.0 48.5 jit_solution(11656645139148280018)
XLA Ops:
  1.3 46.4 %shard_map.77 = (f32[64,256]{1,0:T(8,128)S(1)}, f32[512,256]{1,0:T(8,128)S(1)}) custom-call(s32[1,1,48]{2,1,0:T(1,128)} %users_hbm.1, s32[1,1,48]{2,1,0:T(1,128)} %items_hbm.1, s32[1,1]{1,0:T(1,128)S(6)} %copy.8.counts_hbm, bf16[2048,256]{1,0:T(8,128)(2,1)} %y_hbm.1, f32[256,256]{1,0:T(8,128)} %gram_hbm.1, bf16[48,128,128]{2,1,0:T(8,128)(2,1)} %bitcast.2), custom_call_target="tpu_custom_call" | custom-call | tf_op jit(solution)/shard_map/pallas_call | solution.py:544
  47.7 0.8 %shard_map.78 = (f32[64,256]{1,0:T(8,128)}, f32[512,256]{1,0:T(8,128)}) custom-call(f32[64,256]{1,0:T(8,128)S(1)} %get-tuple-element.6.sol_in, f32[512,256]{1,0:T(8,128)S(1)} %get-tuple-element.7.item_in), custom_call_target="tpu_custom_call" | custom-call | tf_op jit(solution)/shard_map/pallas_call | solution.py:598

commit v4 on v3

--- a/solution.py
+++ b/solution.py
@@ -30,7 +30,7 @@
     nu, ni, scale,
     users_hbm, items_hbm, counts_hbm, y_hbm, gram_hbm, tiles_hbm,
     sol_ref, item_ref,
-    users_in, items_in, count_in, slot_of, inv_ref, tiles, yv, gram, wide, ws, turned, ct, xb, pa, ra, own, sb, rb,
+    users_in, items_in, count_in, slot_of, inv_ref, tiles, yv, gram, wide, ws, turned, ct, xb, pa, ra, own, sb, rb, dn,
     d_state, r_state, x_state, n_state, i_state, a_state, sol_in,
     scal, sums, coef, x2, kept, outgo, income,
     load_sem, w_send, w_recv, a_send, a_recv, y_send, y_recv, b_send, b_recv,
@@ -201,48 +201,41 @@
             mine = [acc[(s * owners + q) * rows : (s * owners + q + 1) * rows] for s in range(STREAMS)]
             sums[o, q : q + 1, 0:per] = jnp.sum(jnp.concatenate(mine, axis=0).T, axis=0, keepdims=True)
 
+    def owner_device(zo):
+        return {"item": zo * 2 + other}
+
     def reduce_start(k, s, total):
-        own[s] = total
         sb[k, s] = total.astype(jnp.bfloat16)
         for i in range(owners):
             q = jnp.where(z * 2 < nz, owners - 1 - i, i)
             zo = q + low
-            j = lax.rem(zo - z + nz, nz)
             part = sb.at[k, s, pl.ds(pl.multiple_of(q * rows, rows), rows)]
-            cp = rcopy(part, rb.at[k, s, j], b_send.at[s, i], b_recv.at[s], {"item": zo * 2 + c})
-            pl.when(z != zo)(cp.start)
+            rcopy(part, rb.at[k, s, lax.rem(zo - z + nz, nz)], b_send.at[s], b_recv.at[s], owner_device(zo)).start()
 
     def reduce_sent(k, s):
-        for i in range(owners):
-            zo = jnp.where(z * 2 < nz, owners - 1 - i, i) + low
-            part = sb.at[k, s, pl.ds(0, rows)]
-            pl.when(z != zo)(rcopy(part, part, b_send.at[s, i], b_recv.at[s], sib).wait_send)
+        rcopy(sb.at[k, s], sb.at[k, s], b_send.at[s], b_recv.at[s], sib).wait_send()
 
     def reduce_end(k, s):
-        total = own[s, pl.ds(pl.multiple_of(place * rows, rows), rows), :]
-        arrived(rb.at[k, s, pl.ds(1, nz - 1)], b_send.at[s, 0], b_recv.at[s], sib)
+        arrived(rb.at[k, s], b_send.at[s], b_recv.at[s], sib)
+        total = rb[k, s, 0].astype(jnp.float32)
         for j in range(1, nz):
             total = total + rb[k, s, j].astype(jnp.float32)
         return total
 
     def gather_send(k, s):
-        mine = xb.at[k, 0, piece(s, place)]
-        for j in zothers:
-            rcopy(mine, mine, z_send.at[s], z_recv.at[s, place], zpeer(j)).start()
+        for j in zothers + [0]:
+            rcopy(
+                dn.at[k, s], xb.at[k, 0, piece(s, place)], z_send.at[s], z_recv.at[s, place],
+                owner_device(lax.rem(z + j, nz)),
+            ).start()
 
     def gather_sent(k, s):
-        every = rb.at[k, s, pl.ds(1, nz - 1)]
-        rcopy(every, every, z_send.at[s], z_recv.at[s, 0], sib).wait_send()
+        rcopy(rb.at[k, s], rb.at[k, s], z_send.at[s], z_recv.at[s, 0], sib).wait_send()
 
     def gather_end(k, s, pass_on):
         for q in range(owners):
-            zo = q + low
             got = xb.at[k, 0, piece(s, q)]
-
-            @pl.when(z != zo)
-            def _():
-                arrived(got, z_send.at[s], z_recv.at[s, q], sib)
-
+            arrived(got, z_send.at[s], z_recv.at[s, q], sib)
             if pass_on:
                 rcopy(got, xb.at[k, 0, piece(s, q, 1)], f_send.at[k], f_recv.at[k], sib).start()
                 for i in range(1, line):
@@ -274,7 +267,7 @@
             r_state[s] = total
             d_state[s] = total
             n_state[s] = jnp.sum(total * total, axis=1, keepdims=True)
-            xb[k, 0, piece(s, place), :] = total.astype(jnp.bfloat16)
+            dn[k, s] = total.astype(jnp.bfloat16)
             return
         direction = d_state[s]
         image = i_state[s] + total
@@ -283,7 +276,7 @@
         residual = r_state[s] - alpha * image
         norm_next = jnp.sum(residual * residual, axis=1, keepdims=True)
         direction_next = residual + norm_next / (norm + epsilon) * direction
-        xb[k, 0, piece(s, place), :] = direction_next.astype(jnp.bfloat16)
+        dn[k, s] = direction_next.astype(jnp.bfloat16)
         moved = alpha * direction
         x_state[s] = moved if k == 1 else x_state[s] + moved
         a_state[k - 1, s] = alpha
@@ -321,7 +314,7 @@
     told = (ni - 1) + 2 * (line - 1) * nz
 
     def scal_slot(t):
-        return scal.at[(t * owners + place) * 2 + c]
+        return scal.at[(t * owners + place) * 2 + other]
 
     def sums_slot(t):
         return sums.at[(t * nz + z) * 2 + c]
@@ -335,7 +328,7 @@
             at = jnp.where(lane == 2, n_state[s], turned)
             at = jnp.where(lane == 1, a_state[1, s], at)
             parts.append(jnp.where(lane == 0, a_state[0, s], at))
-        scal[place * 2 + c, :, 0:per] = jnp.concatenate(parts, axis=0).T[0:8]
+        scal[place * 2 + other, :, 0:per] = jnp.concatenate(parts, axis=0).T[0:8]
         spread(scal_slot, c_send, c_recv, c_recv)
 
     def step(k, s):
@@ -377,13 +370,8 @@
         basis_pass(k - 1)
 
     pl.when(is_owner)(tell)
-    for q in range(owners):
-        for s in range(STREAMS):
-            target = q * STREAMS + s
-            if target != q + low:
-                send_if(
-                    z == q + low, x_state.at[s], sol_in, o_send.at[s], o_recv, {"item": target * 2 + c}
-                )
+    for s in range(STREAMS):
+        send_if(is_owner, x_state.at[s], sol_in, o_send.at[s], o_recv, owner_device(place * STREAMS + s))
     k = ITERS - 1
     for s in range(STREAMS):
         gather_end(k, s, True)
@@ -458,19 +446,14 @@
     for j in range(line):
         kept[j] = jnp.dot(ct[0, j], final, preferred_element_type=jnp.float32)
 
+    arrived(sol_in, o_send.at[0], o_recv, sib)
     for target in range(nz):
-        owner = target // STREAMS + low
         s, q = target % STREAMS, target // STREAMS
 
         @pl.when(z == target)
         def _():
-            if owner == target:
-                before = x_state[s]
-            else:
-                arrived(sol_in, o_send.at[0], o_recv, {"item": owner * 2 + c})
-                before = sol_in[...]
             n = cell(0, 0, q)
-            sol_ref[...] = before + alpha3[s * rows : (s + 1) * rows, n : n + 1] * xb[
+            sol_ref[...] = sol_in[...] + alpha3[s * rows : (s + 1) * rows, n : n + 1] * xb[
                 k, 0, block(0, 0, s, q), :
             ].astype(jnp.float32)
 
@@ -565,6 +548,7 @@
                 vm((STREAMS, srows, rank), f4),
                 vm((ITERS, STREAMS, srows, rank), bf),
                 vm((ITERS, STREAMS, nz, rows, rank), bf),
+                vm((ITERS, STREAMS, rows, rank), bf),
                 vm((STREAMS, rows, rank), f4),
                 vm((STREAMS, rows, rank), f4),
                 vm((STREAMS, rows, rank), f4),
@@ -583,7 +567,7 @@
                 dma(()), dma(()),
                 dma(()), dma(()),
                 dma((2,)), dma((2,)),
-                dma((STREAMS, owners)), dma((STREAMS,)),
+                dma((STREAMS,)), dma((STREAMS,)),
                 dma((STREAMS,)), dma((STREAMS, owners)),
                 dma((ITERS,)), dma((ITERS,)),
                 dma((ITERS,)), dma((ITERS,)),

time: 48.7 us -> 47.4 us (0.973)
  Pallas kernels: 47.2 us -> 46 us
    pallas_call x1, Pallas kernels: 46.4 us -> 45.1 us  [local(): pl.pallas_call(functools.partial(kernel, nu, ni, scale), out_shape=(vm((r...]
where the time goes in v4:
time: 47.4 us; the launch traced here: 47.3 us
  Pallas kernels  46 us (97%)
  between operations  1.29 us (3%)
    pallas_call x1, Pallas kernels, local(): pl.pallas_call(functools.partial(kernel, nu, ni, scale), out_shape=(vm((r...  45.1 us

profile of v4, /device:TPU:0, one launch (start us, length us, event | category | flops | bytes accessed | tf_op | source)
XLA Modules:
  0.0 47.3 jit_solution(9791409537850905047)
XLA Ops:
  1.3 45.1 %shard_map.77 = (f32[64,256]{1,0:T(8,128)S(1)}, f32[512,256]{1,0:T(8,128)S(1)}) custom-call(s32[1,1,48]{2,1,0:T(1,128)} %users_hbm.1, s32[1,1,48]{2,1,0:T(1,128)} %items_hbm.1, s32[1,1]{1,0:T(1,128)S(6)} %copy.8.counts_hbm, bf16[2048,256]{1,0:T(8,128)(2,1)} %y_hbm.1, f32[256,256]{1,0:T(8,128)} %gram_hbm.1, bf16[48,128,128]{2,1,0:T(8,128)(2,1)} %bitcast.2), custom_call_target="tpu_custom_call" | custom-call | tf_op jit(solution)/shard_map/pallas_call | solution.py:527
  46.4 0.8 %shard_map.78 = (f32[64,256]{1,0:T(8,128)}, f32[512,256]{1,0:T(8,128)}) custom-call(f32[64,256]{1,0:T(8,128)S(1)} %get-tuple-element.6.sol_in, f32[512,256]{1,0:T(8,128)S(1)} %get-tuple-element.7.item_in), custom_call_target="tpu_custom_call" | custom-call | tf_op jit(solution)/shard_map/pallas_call | solution.py:582

commit v5 on v4

--- a/solution.py
+++ b/solution.py
@@ -10,27 +10,25 @@
 
 USER_BLK = 4
 ITERS = 3
-CHUNK = 1024
-LAST_CHUNK = 512
+CHUNK = 512
 STREAMS = 2
 LANES = 128
+PIECES = 4
 
 epsilon = 1e-06
 highest = lax.Precision.HIGHEST
 MESH = pl.DeviceIdType.MESH
-NT = (((1,), (1,)), ((), ()))
 
 
 def confidence_of(w):
-    w = w.astype(jnp.float32)
-    return jnp.where(w > 0, 1.0 + w, 0.0).astype(jnp.bfloat16)
+    return jnp.where(w > 0, 1 + w, jnp.zeros_like(w))
 
 
 def kernel(
     nu, ni, scale,
     users_hbm, items_hbm, counts_hbm, y_hbm, gram_hbm, tiles_hbm,
     sol_ref, item_ref,
-    users_in, items_in, count_in, slot_of, inv_ref, tiles, yv, gram, wide, ws, turned, ct, xb, pa, ra, own, sb, rb, dn,
+    users_in, items_in, count_in, slot_of, inv_ref, tiles, yv, yt, gram, wide, ws, turned, ct, xb, pa, ra, own, sb, rb, dn,
     d_state, r_state, x_state, n_state, i_state, a_state, sol_in,
     scal, sums, coef, x2, kept, outgo, income,
     load_sem, w_send, w_recv, a_send, a_recv, y_send, y_recv, b_send, b_recv,
@@ -48,7 +46,6 @@
     srows = owners * rows
     cols = items // nu
     blocks = items // side
-    devices = nu * ni
     per = STREAMS * rows
     g, o = lax.axis_index("user"), lax.axis_index("item")
     z, c = lax.div(o, 2), lax.rem(o, 2)
@@ -77,9 +74,6 @@
 
     def upeer(i, j=0):
         return {"user": unum(i, j)}
-
-    def peer(i):
-        return {"user": lax.rem(g + lax.div(i, ni), nu), "item": lax.rem(o + lax.rem(i, ni), ni)}
 
     def piece(s, q, hh=0):
         at = (hh * STREAMS + s) * srows
@@ -122,12 +116,27 @@
 
     barrier = pltpu.get_barrier_semaphore()
 
-    def greet(i, carry):
-        pl.semaphore_signal(barrier, inc=1, device_id=peer(i), device_id_type=MESH)
+    def signal(dev):
+        pl.semaphore_signal(barrier, inc=1, device_id=dev, device_id_type=MESH)
+
+    def greet(t, carry):
+        signal({"item": lax.rem(o + t, ni)})
         return carry
 
-    lax.fori_loop(1, devices, greet, 0)
-
+    def greet_line(i, t, carry):
+        signal({"user": unum(i, 0), "item": t})
+        return carry
+
+    def greet_cross(i, t, carry):
+        signal({"user": unum(0, i), "item": t * 2 + other})
+        return carry
+
+    lax.fori_loop(1, ni, greet, 0)
+    for i in range(1, line):
+        lax.fori_loop(0, ni, functools.partial(greet_line, i), 0)
+        lax.fori_loop(0, nz, functools.partial(greet_cross, i), 0)
+        signal(upeer(0, i))
+    greeted = (ni - 1) + (line - 1) * (ni + nz + 1)
     tiles[slots] = jnp.zeros((side, side), jnp.bfloat16)
     for cp in index:
         cp.wait()
@@ -140,19 +149,20 @@
     to_scalar.start()
     to_scalar.wait()
     loads[0].wait()
-    for b in range(blocks):
-        for q in range(owners):
-            for s in range(STREAMS):
-                start = (q * STREAMS + s) * 2 * rows
-                u, off = start // side, start % side
-                for hh in range(2):
+    def scatter(hh):
+        for b in range(blocks):
+            for q in range(owners):
+                for s in range(STREAMS):
+                    start = (q * STREAMS + s) * 2 * rows
+                    u, off = start // side, start % side
                     to = ((hh * STREAMS + s) * owners + q) * rows
                     at = pl.ds(pl.multiple_of(off + (c if hh == 0 else other) * rows, rows), rows)
                     wide[to : to + rows, b * side : (b + 1) * side] = tiles[
                         inv_ref[0, u * blocks + b], at, :
                     ]
-    for cp in loads[1:]:
-        cp.wait()
+
+    scatter(1)
+    loads[1].wait()
 
     def wcol(gg):
         return pl.ds(pl.multiple_of(gg * cols, cols), cols)
@@ -165,13 +175,7 @@
 
     def rhs_pass(hh):
         here = slice(hh * half, (hh + 1) * half)
-        acc = jnp.zeros((half, rank), jnp.float32)
-        for i in range(items // CHUNK):
-            at = slice(i * CHUNK, (i + 1) * CHUNK)
-            acc = acc + jnp.dot(
-                confidence_of(wide[here, at]), yv[0, at, :], preferred_element_type=jnp.float32
-            )
-        return acc
+        return jnp.dot(confidence_of(wide[here, :]), yv[0], preferred_element_type=jnp.float32)
 
     def stream_pass(k, s):
         here = slice(s * srows, (s + 1) * srows)
@@ -180,26 +184,35 @@
             for i in range(items // CHUNK):
                 at = slice(i * CHUNK, (i + 1) * CHUNK)
                 yc = yv[side_of, at, :]
-                scores = lax.dot_general(xb[k - 1, 0, here, :], yc, NT, preferred_element_type=jnp.float32)
+                scores = jnp.dot(xb[k - 1, 0, here, :], yt[side_of, :, at], preferred_element_type=jnp.float32)
                 weighted = (scores * w_ref[here, at].astype(jnp.float32)).astype(jnp.bfloat16)
                 acc = acc + jnp.dot(weighted, yc, preferred_element_type=jnp.float32)
         return acc
 
-    def last_pass():
-        acc = jnp.zeros((half, LANES), jnp.float32)
+    def last_pass(s):
+        here = slice(s * srows, (s + 1) * srows)
+        acc = jnp.zeros((srows, LANES), jnp.float32)
         for side_of, w_ref in enumerate((wide, ws)):
-            for i in range(items // LAST_CHUNK):
-                at = slice(i * LAST_CHUNK, (i + 1) * LAST_CHUNK)
-                scores = lax.dot_general(
-                    xb[ITERS - 1, 0, 0:half, :], yv[side_of, at, :], NT, preferred_element_type=jnp.float32
+            for i in range(items // CHUNK):
+                at = slice(i * CHUNK, (i + 1) * CHUNK)
+                scores = jnp.dot(
+                    xb[ITERS - 1, 0, here, :], yt[side_of, :, at], preferred_element_type=jnp.float32
                 )
-                weighted = (scores * w_ref[0:half, at].astype(jnp.float32)).astype(jnp.bfloat16)
+                weighted = (scores * w_ref[here, at].astype(jnp.float32)).astype(jnp.bfloat16)
                 prod = weighted.astype(jnp.float32) * scores
-                for j in range(LAST_CHUNK // LANES):
+                for j in range(CHUNK // LANES):
                     acc = acc + prod[:, j * LANES : (j + 1) * LANES]
+        return acc
+
+    def sums_store(accs):
         for q in range(owners):
-            mine = [acc[(s * owners + q) * rows : (s * owners + q + 1) * rows] for s in range(STREAMS)]
-            sums[o, q : q + 1, 0:per] = jnp.sum(jnp.concatenate(mine, axis=0).T, axis=0, keepdims=True)
+            mine = jnp.concatenate([acc[q * rows : (q + 1) * rows] for acc in accs], axis=0)
+            sums[o, q : q + 1, 0:per] = jnp.sum(mine.T, axis=0, keepdims=True)
+
+    def flip(which):
+        for i in range(items // rank):
+            at = slice(i * rank, (i + 1) * rank)
+            yt[which, :, at] = yv[which, at, :].T
 
     def owner_device(zo):
         return {"item": zo * 2 + other}
@@ -237,7 +250,7 @@
             got = xb.at[k, 0, piece(s, q)]
             arrived(got, z_send.at[s], z_recv.at[s, q], sib)
             if pass_on:
-                rcopy(got, xb.at[k, 0, piece(s, q, 1)], f_send.at[k], f_recv.at[k], sib).start()
+                rcopy(got, xb.at[k, 0, piece(s, q, 1)], f_send.at[k], f_recv.at[k + s], sib).start()
                 for i in range(1, line):
                     rcopy(got, xb.at[k, i, piece(s, q)], u_send.at[k], u_recv.at[k], upeer(i)).start()
 
@@ -248,10 +261,10 @@
         mine = xb.at[k, 0, mine_all]
         rcopy(mine, xb.at[k, 0, theirs_all], f_send.at[k], f_recv.at[k], sib).start()
 
-    def basis_pass(k, which=slice(None)):
+    def basis_pass(k):
         arrived(xb.at[k, 0, theirs_all], f_send.at[k], f_recv.at[k], sib)
         for i in range(1, line):
-            rcopy(xb.at[k, 0, which], xb.at[k, i, which], u_send.at[k], u_recv.at[k], upeer(i)).start()
+            rcopy(xb.at[k, 0], xb.at[k, i], u_send.at[k], u_recv.at[k], upeer(i)).start()
 
     def basis_end(k):
         arrived(xb.at[k, away], u_send.at[k], u_recv.at[k], sib)
@@ -296,7 +309,6 @@
             rcopy(slot(0), slot(0), ss, near, dev).start()
             return carry
 
-        lax.fori_loop(1, ni, column, 0)
         for e in range(2):
             for t in range(1, line):
                 gg = grid(gx + t, gy) if e == 0 else grid(gx, gy + t)
@@ -307,6 +319,7 @@
                     return carry
 
                 lax.fori_loop(0, nz, across, 0)
+        lax.fori_loop(1, ni, column, 0)
 
     def spread_end(every, ss, rs):
         rcopy(every, every, ss, rs, sib).wait_send()
@@ -336,8 +349,9 @@
         gather_send(k, s)
 
     pa[...] = rhs_pass(1)
-    pl.semaphore_wait(barrier, devices - 1)
+    pl.semaphore_wait(barrier, greeted)
     send(pa, ra, a_send, a_recv, sib)
+    scatter(0)
     first = rhs_pass(0)
     for s in range(STREAMS):
         own[s] = first[s * srows : (s + 1) * srows]
@@ -349,11 +363,14 @@
     for i in range(1, line):
         for j in range(line):
             turn(i, j)
+    for j in range(line):
+        turn(0, j)
+    flip(0)
+    loads[2].wait()
+    arrived(yv.at[1], y_send.at[0], y_recv.at[0], sib)
+    flip(1)
     for s in range(STREAMS):
         pl.when(is_owner)(functools.partial(step, 0, s))
-    for j in range(line):
-        turn(0, j)
-    arrived(yv.at[1], y_send.at[0], y_recv.at[0], sib)
     arrived(ws, y_send.at[1], y_recv.at[1], sib)
 
     for k in range(1, ITERS):
@@ -373,11 +390,22 @@
     for s in range(STREAMS):
         send_if(is_owner, x_state.at[s], sol_in, o_send.at[s], o_recv, owner_device(place * STREAMS + s))
     k = ITERS - 1
+
+    def last_forward(s):
+        got = xb.at[k, 0, pl.ds(half + s * srows, srows)]
+        arrived(got, f_send.at[k], f_recv.at[k + s], sib)
+        for i in range(1, line):
+            rcopy(got, xb.at[k, i, pl.ds(half + s * srows, srows)], u_send.at[k], u_recv.at[k], upeer(i)).start()
+
+    rowsums = []
     for s in range(STREAMS):
         gather_end(k, s, True)
-    last_pass()
+        if s:
+            last_forward(s - 1)
+        rowsums.append(last_pass(s))
+    sums_store(rowsums)
     spread(sums_slot, p_send, p_recv.at[0], p_recv.at[1])
-    basis_pass(k, theirs_all)
+    last_forward(STREAMS - 1)
     known = line * owners * 2
 
     @pl.when(is_owner)
@@ -463,14 +491,19 @@
     basis_end(k)
     finals = [final_of(v, alpha3) for v in range(1, line)]
     for j in list(range(1, line)) + [0]:
-        total = kept[j]
-        for v in range(1, line):
-            total = total + jnp.dot(ct[v, j], finals[v - 1], preferred_element_type=jnp.float32)
-        if j:
-            outgo[j - 1] = total.astype(jnp.bfloat16)
-            rcopy(outgo.at[j - 1], income.at[j - 1], r_send, r_recv, upeer(0, j)).start()
-        else:
-            item_ref[...] = total
+        for i in range(PIECES):
+            at = slice(i * cols // PIECES, (i + 1) * cols // PIECES)
+            total = kept[j, at, :]
+            for v in range(1, line):
+                total = total + jnp.dot(ct[v, j, at, :], finals[v - 1], preferred_element_type=jnp.float32)
+            if j:
+                outgo[j - 1, at, :] = total.astype(jnp.bfloat16)
+                part = pl.ds(i * cols // PIECES, cols // PIECES)
+                rcopy(
+                    outgo.at[j - 1, part], income.at[j - 1, part], r_send, r_recv, upeer(0, j)
+                ).start()
+            else:
+                item_ref[at, :] = total
     arrived(income, r_send, r_recv, sib)
     total = item_ref[...]
     for j in range(line - 1):
@@ -537,6 +570,7 @@
                 pltpu.SMEM((8, LANES), jnp.int32),
                 vm((slots + 1, side, side), bf),
                 vm((2, items, rank), bf),
+                vm((2, rank, items), bf),
                 vm((rank, rank), f4),
                 vm((group, items), bf),
                 vm((half, items), bf),
@@ -569,7 +603,7 @@
                 dma((2,)), dma((2,)),
                 dma((STREAMS,)), dma((STREAMS,)),
                 dma((STREAMS,)), dma((STREAMS, owners)),
-                dma((ITERS,)), dma((ITERS,)),
+                dma((ITERS,)), dma((ITERS - 1 + STREAMS,)),
                 dma((ITERS,)), dma((ITERS,)),
                 dma((STREAMS,)), dma(()),
                 dma(()), dma(()), dma(()), dma((2,)),

time: 47.4 us -> 46.1 us (0.973)
  Pallas kernels: 46 us -> 44.6 us
    pallas_call x1, Pallas kernels: 45.1 us -> 43.8 us  [local(): pl.pallas_call(functools.partial(kernel, nu, ni, scale), out_shape=(vm((r...]
where the time goes in v5:
time: 46.1 us; the launch traced here: 45.9 us
  Pallas kernels  44.6 us (97%)
  between operations  1.29 us (3%)
    pallas_call x1, Pallas kernels, local(): pl.pallas_call(functools.partial(kernel, nu, ni, scale), out_shape=(vm((r...  43.8 us

profile of v5, /device:TPU:0, one launch (start us, length us, event | category | flops | bytes accessed | tf_op | source)
XLA Modules:
  0.0 45.9 jit_solution(6564210296835164850)
XLA Ops:
  1.3 43.8 %shard_map.77 = (f32[64,256]{1,0:T(8,128)S(1)}, f32[512,256]{1,0:T(8,128)S(1)}) custom-call(s32[1,1,48]{2,1,0:T(1,128)} %users_hbm.1, s32[1,1,48]{2,1,0:T(1,128)} %items_hbm.1, s32[1,1]{1,0:T(1,128)S(6)} %copy.8.counts_hbm, bf16[2048,256]{1,0:T(8,128)(2,1)} %y_hbm.1, f32[256,256]{1,0:T(8,128)} %gram_hbm.1, bf16[48,128,128]{2,1,0:T(8,128)(2,1)} %bitcast.2), custom_call_target="tpu_custom_call" | custom-call | tf_op jit(solution)/shard_map/pallas_call | solution.py:560
  45.1 0.8 %shard_map.78 = (f32[64,256]{1,0:T(8,128)}, f32[512,256]{1,0:T(8,128)}) custom-call(f32[64,256]{1,0:T(8,128)S(1)} %get-tuple-element.6.sol_in, f32[512,256]{1,0:T(8,128)S(1)} %get-tuple-element.7.item_in), custom_call_target="tpu_custom_call" | custom-call | tf_op jit(solution)/shard_map/pallas_call | solution.py:616

commit v6 on v5

--- a/solution.py
+++ b/solution.py
@@ -12,6 +12,7 @@
 ITERS = 3
 CHUNK = 512
 STREAMS = 2
+PARTS = 2
 LANES = 128
 PIECES = 4
 
@@ -217,28 +218,35 @@
     def owner_device(zo):
         return {"item": zo * 2 + other}
 
+    parts = rb.shape[2]
+    prows = rows // parts
+
     def reduce_start(k, s, total):
         sb[k, s] = total.astype(jnp.bfloat16)
-        for i in range(owners):
-            q = jnp.where(z * 2 < nz, owners - 1 - i, i)
-            zo = q + low
-            part = sb.at[k, s, pl.ds(pl.multiple_of(q * rows, rows), rows)]
-            rcopy(part, rb.at[k, s, lax.rem(zo - z + nz, nz)], b_send.at[s], b_recv.at[s], owner_device(zo)).start()
+        for t in range(parts):
+            for i in range(owners):
+                q = jnp.where(z * 2 < nz, owners - 1 - i, i)
+                zo = q + low
+                part = sb.at[k, s, pl.ds(pl.multiple_of(q * rows + t * prows, prows), prows)]
+                to = rb.at[k, s, t, lax.rem(zo - z + nz, nz)]
+                rcopy(part, to, b_send.at[s], b_recv.at[s, t], owner_device(zo)).start()
 
     def reduce_sent(k, s):
-        rcopy(sb.at[k, s], sb.at[k, s], b_send.at[s], b_recv.at[s], sib).wait_send()
-
-    def reduce_end(k, s):
-        arrived(rb.at[k, s], b_send.at[s], b_recv.at[s], sib)
-        total = rb[k, s, 0].astype(jnp.float32)
+        rcopy(sb.at[k, s], sb.at[k, s], b_send.at[s], b_recv.at[s, 0], sib).wait_send()
+
+    def reduce_end(k, s, t):
+        arrived(rb.at[k, s, t], b_send.at[s], b_recv.at[s, t], sib)
+        total = rb[k, s, t, 0].astype(jnp.float32)
         for j in range(1, nz):
-            total = total + rb[k, s, j].astype(jnp.float32)
+            total = total + rb[k, s, t, j].astype(jnp.float32)
         return total
 
-    def gather_send(k, s):
+    def gather_send(k, s, t):
+        part = pl.ds(t * prows, prows)
+        at = pl.ds(pl.multiple_of(s * srows + place * rows + t * prows, prows), prows)
         for j in zothers + [0]:
             rcopy(
-                dn.at[k, s], xb.at[k, 0, piece(s, place)], z_send.at[s], z_recv.at[s, place],
+                dn.at[k, s, part], xb.at[k, 0, at], z_send.at[s], z_recv.at[s, place],
                 owner_device(lax.rem(z + j, nz)),
             ).start()
 
@@ -274,28 +282,30 @@
         rcopy(mine, mine, f_send.at[k], f_recv.at[k], sib).wait_send()
         rcopy(got, got, u_send.at[k], u_recv.at[k], sib).wait_send()
 
-    def update(k, s):
-        total = reduce_end(k, s)
+    def update(k, s, t):
+        at = slice(t * prows, (t + 1) * prows)
+        total = reduce_end(k, s, t)
         if k == 0:
-            r_state[s] = total
-            d_state[s] = total
-            n_state[s] = jnp.sum(total * total, axis=1, keepdims=True)
-            dn[k, s] = total.astype(jnp.bfloat16)
+            r_state[s, at] = total
+            d_state[s, at] = total
+            n_state[s, at] = jnp.sum(total * total, axis=1, keepdims=True)
+            dn[k, s, at] = total.astype(jnp.bfloat16)
             return
-        direction = d_state[s]
-        image = i_state[s] + total
-        norm = n_state[s]
+        direction = d_state[s, at]
+        image = i_state[s, at] + total
+        norm = n_state[s, at]
         alpha = norm / (jnp.sum(direction * image, axis=1, keepdims=True) + epsilon)
-        residual = r_state[s] - alpha * image
+        residual = r_state[s, at] - alpha * image
         norm_next = jnp.sum(residual * residual, axis=1, keepdims=True)
         direction_next = residual + norm_next / (norm + epsilon) * direction
-        dn[k, s] = direction_next.astype(jnp.bfloat16)
+        dn[k, s, at] = direction_next.astype(jnp.bfloat16)
+        gather_send(k, s, t)
         moved = alpha * direction
-        x_state[s] = moved if k == 1 else x_state[s] + moved
-        a_state[k - 1, s] = alpha
-        r_state[s] = residual
-        d_state[s] = direction_next
-        n_state[s] = norm_next
+        x_state[s, at] = moved if k == 1 else x_state[s, at] + moved
+        a_state[k - 1, s, at] = alpha
+        r_state[s, at] = residual
+        d_state[s, at] = direction_next
+        n_state[s, at] = norm_next
 
     def grams():
         for s in range(STREAMS):
@@ -345,8 +355,10 @@
         spread(scal_slot, c_send, c_recv, c_recv)
 
     def step(k, s):
-        update(k, s)
-        gather_send(k, s)
+        for t in range(parts):
+            update(k, s, t)
+            if k == 0:
+                gather_send(k, s, t)
 
     pa[...] = rhs_pass(1)
     pl.semaphore_wait(barrier, greeted)
@@ -554,6 +566,7 @@
         dma = pltpu.SemaphoreType.DMA
         vm = pltpu.VMEM
         line = math.isqrt(nu)
+        parts = min(PARTS, rows // 16)
         cells = max(8, line * 2 * owners)
         anywhere = pl.BlockSpec(memory_space=pl.ANY)
         vmem = pl.BlockSpec(memory_space=pltpu.VMEM)
@@ -581,7 +594,7 @@
                 vm((half, rank), f4),
                 vm((STREAMS, srows, rank), f4),
                 vm((ITERS, STREAMS, srows, rank), bf),
-                vm((ITERS, STREAMS, nz, rows, rank), bf),
+                vm((ITERS, STREAMS, parts, nz, rows // parts, rank), bf),
                 vm((ITERS, STREAMS, rows, rank), bf),
                 vm((STREAMS, rows, rank), f4),
                 vm((STREAMS, rows, rank), f4),
@@ -601,7 +614,7 @@
                 dma(()), dma(()),
                 dma(()), dma(()),
                 dma((2,)), dma((2,)),
-                dma((STREAMS,)), dma((STREAMS,)),
+                dma((STREAMS,)), dma((STREAMS, parts)),
                 dma((STREAMS,)), dma((STREAMS, owners)),
                 dma((ITERS,)), dma((ITERS - 1 + STREAMS,)),
                 dma((ITERS,)), dma((ITERS,)),

time: 46.1 us -> 45.1 us (0.978)
  Pallas kernels: 44.6 us -> 43.7 us
    pallas_call x1, Pallas kernels: 43.8 us -> 42.9 us  [local(): pl.pallas_call(functools.partial(kernel, nu, ni, scale), out_shape=(vm((r...]
where the time goes in v6:
time: 45.1 us; the launch traced here: 45 us
  Pallas kernels  43.7 us (97%)
  between operations  1.29 us (3%)
    pallas_call x1, Pallas kernels, local(): pl.pallas_call(functools.partial(kernel, nu, ni, scale), out_shape=(vm((r...  42.9 us

profile of v6, /device:TPU:0, one launch (start us, length us, event | category | flops | bytes accessed | tf_op | source)
XLA Modules:
  0.0 45.0 jit_solution(14380874988812993501)
XLA Ops:
  1.3 42.9 %shard_map.77 = (f32[64,256]{1,0:T(8,128)S(1)}, f32[512,256]{1,0:T(8,128)S(1)}) custom-call(s32[1,1,48]{2,1,0:T(1,128)} %users_hbm.1, s32[1,1,48]{2,1,0:T(1,128)} %items_hbm.1, s32[1,1]{1,0:T(1,128)S(6)} %copy.8.counts_hbm, bf16[2048,256]{1,0:T(8,128)(2,1)} %y_hbm.1, f32[256,256]{1,0:T(8,128)} %gram_hbm.1, bf16[48,128,128]{2,1,0:T(8,128)(2,1)} %bitcast.2), custom_call_target="tpu_custom_call" | custom-call | tf_op jit(solution)/shard_map/pallas_call | solution.py:573
  44.2 0.8 %shard_map.78 = (f32[64,256]{1,0:T(8,128)}, f32[512,256]{1,0:T(8,128)}) custom-call(f32[64,256]{1,0:T(8,128)S(1)} %get-tuple-element.6.sol_in, f32[512,256]{1,0:T(8,128)S(1)} %get-tuple-element.7.item_in), custom_call_target="tpu_custom_call" | custom-call | tf_op jit(solution)/shard_map/pallas_call | solution.py:629

commit v7 on v6

--- a/solution.py
+++ b/solution.py
@@ -76,6 +76,9 @@
     def upeer(i, j=0):
         return {"user": unum(i, j)}
 
+    def cross(i):
+        return {"user": unum(0, i), "item": z * 2 + other}
+
     def piece(s, q, hh=0):
         at = (hh * STREAMS + s) * srows
         if isinstance(q, int):
@@ -199,8 +202,7 @@
                 scores = jnp.dot(
                     xb[ITERS - 1, 0, here, :], yt[side_of, :, at], preferred_element_type=jnp.float32
                 )
-                weighted = (scores * w_ref[here, at].astype(jnp.float32)).astype(jnp.bfloat16)
-                prod = weighted.astype(jnp.float32) * scores
+                prod = scores * (scores * w_ref[here, at].astype(jnp.float32))
                 for j in range(CHUNK // LANES):
                     acc = acc + prod[:, j * LANES : (j + 1) * LANES]
         return acc
@@ -261,6 +263,7 @@
                 rcopy(got, xb.at[k, 0, piece(s, q, 1)], f_send.at[k], f_recv.at[k + s], sib).start()
                 for i in range(1, line):
                     rcopy(got, xb.at[k, i, piece(s, q)], u_send.at[k], u_recv.at[k], upeer(i)).start()
+                    rcopy(got, xb.at[k, i, piece(s, q, 1)], u_send.at[k], u_recv.at[k], cross(i)).start()
 
     mine_all, theirs_all = pl.ds(0, half), pl.ds(half, half)
     away = pl.ds(1, line - 1)
@@ -268,11 +271,9 @@
     def basis_send(k):
         mine = xb.at[k, 0, mine_all]
         rcopy(mine, xb.at[k, 0, theirs_all], f_send.at[k], f_recv.at[k], sib).start()
-
-    def basis_pass(k):
-        arrived(xb.at[k, 0, theirs_all], f_send.at[k], f_recv.at[k], sib)
         for i in range(1, line):
-            rcopy(xb.at[k, 0], xb.at[k, i], u_send.at[k], u_recv.at[k], upeer(i)).start()
+            rcopy(mine, xb.at[k, i, mine_all], u_send.at[k], u_recv.at[k], upeer(i)).start()
+            rcopy(mine, xb.at[k, i, theirs_all], u_send.at[k], u_recv.at[k], cross(i)).start()
 
     def basis_end(k):
         arrived(xb.at[k, away], u_send.at[k], u_recv.at[k], sib)
@@ -396,28 +397,22 @@
         for s in range(STREAMS):
             pl.when(is_owner)(functools.partial(gather_sent, k - 1, s))
             pl.when(is_owner)(functools.partial(step, k, s))
-        basis_pass(k - 1)
 
     pl.when(is_owner)(tell)
     for s in range(STREAMS):
         send_if(is_owner, x_state.at[s], sol_in, o_send.at[s], o_recv, owner_device(place * STREAMS + s))
     k = ITERS - 1
 
-    def last_forward(s):
+    def last_theirs(s):
         got = xb.at[k, 0, pl.ds(half + s * srows, srows)]
         arrived(got, f_send.at[k], f_recv.at[k + s], sib)
-        for i in range(1, line):
-            rcopy(got, xb.at[k, i, pl.ds(half + s * srows, srows)], u_send.at[k], u_recv.at[k], upeer(i)).start()
 
     rowsums = []
     for s in range(STREAMS):
         gather_end(k, s, True)
-        if s:
-            last_forward(s - 1)
         rowsums.append(last_pass(s))
     sums_store(rowsums)
     spread(sums_slot, p_send, p_recv.at[0], p_recv.at[1])
-    last_forward(STREAMS - 1)
     known = line * owners * 2
 
     @pl.when(is_owner)
@@ -448,6 +443,7 @@
         coef[0:4, n, :] = scal[(v * owners + q) * 2 + cc][0:4]
     alpha1, alpha2 = coef[0].T, coef[1].T
     for j in range(k):
+        arrived(xb.at[j, 0, theirs_all], f_send.at[j], f_recv.at[j], sib)
         basis_end(j)
     for v, hh, q, cc in cells(every):
         n = cell(v, hh, q)
@@ -482,6 +478,8 @@
 
     arrived(sums.at[pl.ds(0, ni - 1)], p_send, p_recv.at[0], sib)
     alpha3 = alphas([0])
+    for s in range(STREAMS):
+        last_theirs(s)
     final = final_of(0, alpha3)
     for j in range(line):
         kept[j] = jnp.dot(ct[0, j], final, preferred_element_type=jnp.float32)

time: 45.1 us -> 45 us (level)
  no operation moved by 1% of the time
where the time goes in v7:
time: 45 us; the launch traced here: 44.8 us
  Pallas kernels  43.5 us (97%)
  between operations  1.29 us (3%)
    pallas_call x1, Pallas kernels, local(): pl.pallas_call(functools.partial(kernel, nu, ni, scale), out_shape=(vm((r...  42.7 us

profile of v7, /device:TPU:0, one launch (start us, length us, event | category | flops | bytes accessed | tf_op | source)
XLA Modules:
  0.0 44.8 jit_solution(13901661789666505224)
XLA Ops:
  1.3 42.7 %shard_map.77 = (f32[64,256]{1,0:T(8,128)S(1)}, f32[512,256]{1,0:T(8,128)S(1)}) custom-call(s32[1,1,48]{2,1,0:T(1,128)} %users_hbm.1, s32[1,1,48]{2,1,0:T(1,128)} %items_hbm.1, s32[1,1]{1,0:T(1,128)S(6)} %copy.8.counts_hbm, bf16[2048,256]{1,0:T(8,128)(2,1)} %y_hbm.1, f32[256,256]{1,0:T(8,128)} %gram_hbm.1, bf16[48,128,128]{2,1,0:T(8,128)(2,1)} %bitcast.2), custom_call_target="tpu_custom_call" | custom-call | tf_op jit(solution)/shard_map/pallas_call | solution.py:571
  44.0 0.8 %shard_map.78 = (f32[64,256]{1,0:T(8,128)}, f32[512,256]{1,0:T(8,128)}) custom-call(f32[64,256]{1,0:T(8,128)S(1)} %get-tuple-element.6.sol_in, f32[512,256]{1,0:T(8,128)S(1)} %get-tuple-element.7.item_in), custom_call_target="tpu_custom_call" | custom-call | tf_op jit(solution)/shard_map/pallas_call | solution.py:627

commit v8 on v7

--- a/solution.py
+++ b/solution.py
@@ -363,15 +363,17 @@
 
     pa[...] = rhs_pass(1)
     pl.semaphore_wait(barrier, greeted)
-    send(pa, ra, a_send, a_recv, sib)
+    for s in range(STREAMS):
+        here = pl.ds(s * srows, srows)
+        send(pa.at[here], ra.at[here], a_send.at[s], a_recv.at[s], sib)
     scatter(0)
     first = rhs_pass(0)
     for s in range(STREAMS):
         own[s] = first[s * srows : (s + 1) * srows]
     send(yv.at[0], yv.at[1], y_send.at[0], y_recv.at[0], sib)
     send(wide.at[theirs_all], ws, y_send.at[1], y_recv.at[1], sib)
-    arrived(ra, a_send, a_recv, sib)
-    for s in range(STREAMS):
+    for s in range(STREAMS):
+        arrived(ra.at[pl.ds(s * srows, srows)], a_send.at[s], a_recv.at[s], sib)
         reduce_start(0, s, own[s] + ra[s * srows : (s + 1) * srows, :])
     for i in range(1, line):
         for j in range(line):
@@ -610,7 +612,7 @@
                 vm((line - 1, cols, rank), bf),
                 dma((7,)),
                 dma(()), dma(()),
-                dma(()), dma(()),
+                dma((STREAMS,)), dma((STREAMS,)),
                 dma((2,)), dma((2,)),
                 dma((STREAMS,)), dma((STREAMS, parts)),
                 dma((STREAMS,)), dma((STREAMS, owners)),

time: 45 us -> 44.8 us (level)
  no operation moved by 1% of the time
where the time goes in v8:
time: 44.8 us; the launch traced here: 44.6 us
  Pallas kernels  43.3 us (97%)
  between operations  1.29 us (3%)
    pallas_call x1, Pallas kernels, local(): pl.pallas_call(functools.partial(kernel, nu, ni, scale), out_shape=(vm((r...  42.5 us

profile of v8, /device:TPU:0, one launch (start us, length us, event | category | flops | bytes accessed | tf_op | source)
XLA Modules:
  0.0 44.6 jit_solution(11633086680363949304)
XLA Ops:
  1.3 42.5 %shard_map.77 = (f32[64,256]{1,0:T(8,128)S(1)}, f32[512,256]{1,0:T(8,128)S(1)}) custom-call(s32[1,1,48]{2,1,0:T(1,128)} %users_hbm.1, s32[1,1,48]{2,1,0:T(1,128)} %items_hbm.1, s32[1,1]{1,0:T(1,128)S(6)} %copy.8.counts_hbm, bf16[2048,256]{1,0:T(8,128)(2,1)} %y_hbm.1, f32[256,256]{1,0:T(8,128)} %gram_hbm.1, bf16[48,128,128]{2,1,0:T(8,128)(2,1)} %bitcast.2), custom_call_target="tpu_custom_call" | custom-call | tf_op jit(solution)/shard_map/pallas_call | solution.py:573
  43.8 0.8 %shard_map.78 = (f32[64,256]{1,0:T(8,128)}, f32[512,256]{1,0:T(8,128)}) custom-call(f32[64,256]{1,0:T(8,128)S(1)} %get-tuple-element.6.sol_in, f32[512,256]{1,0:T(8,128)S(1)} %get-tuple-element.7.item_in), custom_call_target="tpu_custom_call" | custom-call | tf_op jit(solution)/shard_map/pallas_call | solution.py:629
